TPU v7x, 256 devices: a whole 4x4x8 slice. The times are simulated.
256 devices in a mesh: seq: 32 (over x, z), expert: 8 (over y, core).
Axes of the slice: x: 4, y: 4, z: 8, core: 2. Of those that a mesh axis runs over, the one named last changes fastest.
Arguments:
- byte_states: bfloat16 [65536, 512], P(('seq', 'expert')), may hold values from -6 to 6
- patch_start: int32 [65536], P(('seq', 'expert')), may hold values from 0 to 1, as said below
- expert_ids: int32 [10240, 2], P(('seq', 'expert')), may hold values from 0 to 7, all different within a row; in each aligned block of 40 rows (0 to 39, 40 to 79, ...) at most 12 rows name the same one
- enc_gain: float32 [512], replicated, may hold values from 0.1 to 1.9
- w_qkv: bfloat16 [512, 1536], replicated, may hold values from -0.25 to 0.25
- w_out: bfloat16 [512, 512], replicated, may hold values from -0.25 to 0.25
- w_xq: bfloat16 [512, 512], replicated, may hold values from -0.25 to 0.25
- w_xkv: bfloat16 [512, 1024], replicated, may hold values from -0.25 to 0.25
- w_up: bfloat16 [512, 2048], replicated, may hold values from -0.25 to 0.25
- moe_gain: float32 [2048], replicated, may hold values from 0.1 to 1.9
- w_router: float32 [2048, 8], replicated, may hold values from -0.03125 to 0.03125
- w_in: bfloat16 [8, 2048, 2, 6144], P('expert', None, None, 'seq'), may hold values from -0.125 to 0.125
- w_down: bfloat16 [8, 6144, 2048], P('expert', 'seq'), may hold values from -0.15625 to 0.15625
- dec_gain: float32 [512], replicated, may hold values from 0.1 to 1.9
- w_dq: bfloat16 [512, 512], replicated, may hold values from -0.25 to 0.25
- w_dkv: bfloat16 [2048, 1024], replicated, may hold values from -0.125 to 0.125
- w_do: bfloat16 [512, 512], replicated, may hold values from -0.25 to 0.25
Outputs:
- bytes_out: bfloat16 [65536, 512], P(('seq', 'expert'))
- patch_out: bfloat16 [10240, 2048], P(('seq', 'expert'))
Inputs may be any that keep to these rules, and one draw needn't show every extreme that they name: `patch_start`: the first byte of every block of 256 bytes has a 1; every block has between 20 and 40 ones, and some block has exactly 40. `expert_ids`: the two experts of a slot differ. Among the 80 entries of one block's slots no expert appears more than 12 times, and some expert appears exactly 12 times in some block.
All inputs are finite; a program needn't handle non-finite values.
Results may differ from a plain program's by a relative error of at most 0.025.
Values may be sent and summed in bfloat16 or wider, within the bound.
A program may use at most 128 MiB of HBM per device.

v0:
```python
import math

import jax
import jax.numpy as jnp
from jax import lax
from jax.sharding import Mesh
from jax.sharding import PartitionSpec as P

HEADS_L = 8
HEAD = 64
WINDOW = 512
SEQ = ("seq_0", "seq_1")
SEQ_EXPERT = ("seq_0", "seq_1", "expert")


epsilon = 1e-06
very_negative = -1e30


def own_rows(terms, axes):
    subtotal = terms.astype(jnp.bfloat16)
    for axis in axes:
        subtotal = lax.psum_scatter(subtotal, axis, scatter_dimension=0, tiled=True)
    return subtotal.astype(jnp.float32)


def passed_along(x, axis, by):
    length = lax.axis_size(axis)
    pairs = [(i, i + by) for i in range(length) if 0 <= i + by < length]
    return lax.ppermute(x, axis, pairs)


def rms_scale(inputs, gain_vector):
    widened = inputs.astype(jnp.float32)
    return (
        widened
        * lax.rsqrt(jnp.mean(widened * widened, axis=-1, keepdims=True) + epsilon)
        * gain_vector
    )


def softmax_rows(scores):
    highest = jnp.max(scores, axis=-1, keepdims=True)
    raised = jnp.exp(scores - highest)
    return raised / jnp.sum(raised, axis=-1, keepdims=True)


def heads_split(inputs):
    return inputs.reshape(inputs.shape[0], HEADS_L, HEAD).transpose(1, 0, 2)


def heads_merge(inputs):
    return inputs.transpose(1, 0, 2).reshape(inputs.shape[1], HEADS_L * HEAD)


def attend(queries, keys, values, allowed):
    scores = jnp.einsum(
        "hqd,hkd->hqk", queries, keys, preferred_element_type=jnp.float32
    ) / math.sqrt(HEAD)
    scores = jnp.where(allowed[None], scores, very_negative)
    weights = softmax_rows(scores).astype(jnp.bfloat16)
    mixed = jnp.einsum("hqk,hkd->hqd", weights, values, preferred_element_type=jnp.float32)
    return heads_merge(mixed)


def window_mask(query_place, key_place):
    later = key_place[None, :]
    return (later >= 0) & (later <= query_place[:, None]) & (later > query_place[:, None] - WINDOW)


def patch_block(encoded, flags, w_xq, w_xkv, w_up):
    patch_cap = encoded.shape[0] * 5 // 32
    patch_index = jnp.cumsum(flags) - 1
    patch_count = jnp.sum(flags)
    slot_list = jnp.arange(patch_cap, dtype=jnp.int32)
    member = patch_index[None, :] == slot_list[:, None]
    live = slot_list < patch_count
    pooled = jnp.max(
        jnp.where(member[:, :, None], encoded[None], jnp.asarray(very_negative, encoded.dtype)),
        axis=1,
    )
    pooled = jnp.where(live[:, None], pooled, jnp.zeros_like(pooled))
    queries = jnp.dot(pooled, w_xq, preferred_element_type=jnp.float32).astype(jnp.bfloat16)
    pairs = jnp.dot(encoded, w_xkv, preferred_element_type=jnp.float32).astype(jnp.bfloat16)
    width_local = pairs.shape[1] // 2
    mixed = attend(
        heads_split(queries),
        heads_split(pairs[:, :width_local]),
        heads_split(pairs[:, width_local:]),
        member,
    )
    patch_input = (pooled.astype(jnp.float32) + mixed).astype(jnp.bfloat16)
    state = jnp.dot(patch_input, w_up, preferred_element_type=jnp.float32)
    return jnp.where(live[:, None], state, jnp.zeros_like(state)).astype(jnp.bfloat16)


def decode_block(encoded, flags, states, dec_gain, w_dq, w_dkv, w_do):
    patch_index = jnp.cumsum(flags) - 1
    slot_list = jnp.arange(states.shape[0], dtype=jnp.int32)
    normed = rms_scale(encoded, dec_gain).astype(jnp.bfloat16)
    queries = jnp.dot(normed, w_dq, preferred_element_type=jnp.float32).astype(jnp.bfloat16)
    pairs = jnp.dot(states, w_dkv, preferred_element_type=jnp.float32).astype(jnp.bfloat16)
    width_local = pairs.shape[1] // 2
    allowed = slot_list[None, :] <= patch_index[:, None]
    mixed = attend(
        heads_split(queries),
        heads_split(pairs[:, :width_local]),
        heads_split(pairs[:, width_local:]),
        allowed,
    ).astype(jnp.bfloat16)
    return (
        encoded.astype(jnp.float32) + jnp.dot(mixed, w_do, preferred_element_type=jnp.float32)
    ).astype(jnp.bfloat16)


def route_slots(expert_ids, experts):
    flat = expert_ids.reshape(-1)
    onehot = (flat[:, None] == jnp.arange(experts, dtype=jnp.int32)[None, :]).astype(jnp.int32)
    ranked = jnp.cumsum(onehot, axis=0) - 1
    return jnp.sum(ranked * onehot, axis=1).reshape(expert_ids.shape)


def mixture(patch_state, expert_ids, moe_gain, w_router, w_in, w_down):
    patch_cap = patch_state.shape[0]
    global_width = patch_state.shape[1]
    experts = w_router.shape[1]
    local_experts = w_in.shape[0]
    expert_devices = experts // local_experts
    capacity = 12 * patch_cap // (5 * experts)
    hidden_share = w_in.shape[3]
    normed = rms_scale(patch_state, moe_gain).astype(jnp.bfloat16)
    logits = jnp.dot(normed.astype(jnp.float32), w_router, precision=lax.Precision.HIGHEST)
    gates = softmax_rows(jnp.take_along_axis(logits, expert_ids, axis=1))
    slot_number = route_slots(expert_ids, experts)
    target = (
        expert_ids // local_experts * capacity + slot_number
    ) * local_experts + expert_ids % local_experts
    places = jnp.arange(experts * capacity, dtype=jnp.int32)
    dispatch = jnp.sum((target[None, :, :] == places[:, None, None]).astype(jnp.bfloat16), axis=2)
    routed = jnp.dot(dispatch, normed, preferred_element_type=jnp.float32).astype(jnp.bfloat16)
    arrived = lax.all_to_all(
        routed.reshape(expert_devices, capacity * local_experts, global_width),
        "expert",
        split_axis=0,
        concat_axis=0,
        tiled=True,
    )
    rows = arrived.reshape(expert_devices * capacity, local_experts, global_width)
    paired = w_in.reshape(local_experts, global_width, 2 * hidden_share)
    both = jnp.einsum(
        "red,edk->rek",
        lax.all_gather(rows, SEQ, axis=0, tiled=True),
        paired,
        preferred_element_type=jnp.float32,
    )
    hidden = (jax.nn.silu(both[..., :hidden_share]) * both[..., hidden_share:]).astype(jnp.bfloat16)
    term = jnp.einsum("ref,efd->red", hidden, w_down, preferred_element_type=jnp.float32).astype(
        jnp.bfloat16
    )
    term = lax.optimization_barrier(term)
    summed = own_rows(term.astype(jnp.float32), SEQ)
    results = summed.astype(jnp.bfloat16).reshape(
        expert_devices, capacity * local_experts, global_width
    )
    returned = lax.all_to_all(results, "expert", split_axis=0, concat_axis=0, tiled=True)
    chosen = returned.reshape(experts * capacity, global_width)[target]
    combined = jnp.sum(gates[..., None] * chosen.astype(jnp.float32), axis=1)
    return (patch_state.astype(jnp.float32) + combined).astype(jnp.bfloat16)


def per_device(
    byte_states,
    patch_start,
    expert_ids,
    enc_gain,
    w_qkv,
    w_out,
    w_xq,
    w_xkv,
    w_up,
    moe_gain,
    w_router,
    w_in,
    w_down,
    dec_gain,
    w_dq,
    w_dkv,
    w_do,
):
    byte_dev = byte_states.shape[0]
    model_width = byte_states.shape[1]
    normed = rms_scale(byte_states, enc_gain).astype(jnp.bfloat16)
    projected = jnp.dot(normed, w_qkv, preferred_element_type=jnp.float32).astype(jnp.bfloat16)
    queries = projected[:, :model_width]
    own_pairs = projected[:, model_width:]
    reach = -(-WINDOW // byte_dev)
    earlier = []
    for distance in range(reach, 0, -1):
        moved = passed_along(normed, SEQ_EXPERT, distance)
        earlier.append(
            jnp.dot(moved, w_qkv[:, model_width:], preferred_element_type=jnp.float32).astype(
                jnp.bfloat16
            )
        )
    pairs = jnp.concatenate(earlier + [own_pairs], axis=0)
    offset = lax.axis_index(SEQ_EXPERT) * byte_dev
    query_place = offset + jnp.arange(byte_dev, dtype=jnp.int32)
    key_place = offset - reach * byte_dev + jnp.arange((reach + 1) * byte_dev, dtype=jnp.int32)
    mixed = attend(
        heads_split(queries),
        heads_split(pairs[:, :model_width]),
        heads_split(pairs[:, model_width:]),
        window_mask(query_place, key_place),
    ).astype(jnp.bfloat16)
    encoded = (
        byte_states.astype(jnp.float32) + jnp.dot(mixed, w_out, preferred_element_type=jnp.float32)
    ).astype(jnp.bfloat16)
    patch_state = patch_block(encoded, patch_start, w_xq, w_xkv, w_up)
    patch_out = mixture(patch_state, expert_ids, moe_gain, w_router, w_in, w_down)
    bytes_out = decode_block(encoded, patch_start, patch_out, dec_gain, w_dq, w_dkv, w_do)
    return (bytes_out, patch_out)


def solution(mesh):
    split = Mesh(mesh.devices.reshape(4, 8, mesh.shape["expert"]), ("seq_0", "seq_1", "expert"))
    placed = (
        P(SEQ_EXPERT, None),
        P(SEQ_EXPERT),
        P(SEQ_EXPERT, None),
        P(),
        P(),
        P(),
        P(),
        P(),
        P(),
        P(),
        P(),
        P("expert", None, None, SEQ),
        P("expert", SEQ, None),
        P(),
        P(),
        P(),
        P(),
    )
    return jax.shard_map(
        per_device,
        mesh=split,
        in_specs=placed,
        out_specs=(P(SEQ_EXPERT, None), P(SEQ_EXPERT, None)),
        check_vma=False,
    )
```

profile of v0, /device:TPU:1, one launch (start us, length us, event | category | flops | bytes accessed | tf_op | source)
XLA Modules:
  0.0 395.4 jit_solution(6304937564906660591)
XLA Ops:
  7.2 1.2 fusion.32
  8.5 1.8 fusion.34
  10.3 4.6 %collective-permute-start.1 = (bf16[256,512]{1,0:T(8,128)(2,1)}, bf16[256,512]{1,0:T(8,128)(2,1)}, u32[]{:S(2)}, u32[]{:S(2)}) collective-permute-start(bf16[256,512]{1,0:T(8,128)(2,1)} %fusion.34), channel_id=1, source_target_pairs={{0,1},{1,2},{2,3},{3,4},{4,5},{5,6},{6,7},{7,8},{8,9},{9,10},{10,1... | collective-permute-start | bytes 786440 | tf_op jit(solution)/shard_map/ppermute | solution.py:30
  14.8 3.9 collective-permute-start
  18.8 2.1 convolution_convert_fusion
  23.8 0.7 slice.58
  24.5 1.8 copy.79
  26.3 1.0 compare_and_fusion
  27.2 1.8 convolution_convert_fusion.3
  29.0 1.8 convolution_convert_fusion.4
  30.9 1.0 fusion.63
  31.9 2.3 copy.80
  34.2 1.1 copy.81
  35.4 6.2 %fusion.66 = (f32[8,256]{1,0:T(8,128)S(1)}, f32[8,256,768]{2,1,0:T(8,128)}) fusion(pred[256,768]{1,0:T(8,128)(4,1)S(1)} %copy-done.7, bf16[8,256,64]{1,2,0:T(8,128)(2,1)S(1)} %bitcast.103, bf16[8,768,64]{1,2,0:T(8,128)(2,1)} %bitcast.100), kind=kOutput, calls=%fused_computation.120 | convolution fusion | flops 207618816 | bytes 7544832 | tf_op jit(solution)/shard_map/sub | solution.py:44
  41.6 4.0 %fusion.20 = bf16[8,256,64]{1,2,0:T(8,128)(2,1)S(1)} fusion(bf16[8,768,64]{1,2,0:T(8,128)(2,1)S(1)} %bitcast.101, f32[8,256,768]{2,1,0:T(8,128)} %get-tuple-element.13, f32[8,256]{1,0:T(8,128)S(1)} %get-tuple-element.12), kind=kOutput, calls=%fused_computation.37 | convolution fusion | flops 204603392 | bytes 7348224 | tf_op jit(solution)/shard_map/hqk,hkd->hqd/dot_general | solution.py:62
  46.0 1.8 select_reduce_fusion
  48.3 1.7 convolution_convert_fusion.2
  52.5 12.9 %all_to_all.10 = bf16[8,12,2048]{2,1,0:T(8,128)(2,1)S(1)} all-to-all(bf16[8,12,2048]{2,1,0:T(8,128)(2,1)S(1)} %reshape.331), channel_id=1, replica_groups=mesh['seq_0'=4,'seq_1'=8,'expert'=8] {'expert'}, dimensions={0} | all-to-all | bytes 786432 | tf_op jit(solution)/shard_map/all_to_all | solution.py:141
  65.4 0.9 reshape.332
  66.5 118.3 %all-gather.2.cloned.1.call-done = bf16[3072,1,2048]{2,0,1:T(8,128)(2,1)} async-done(((bf16[96,1,2048]{2,0,1:T(8,128)(2,1)}), bf16[3072,1,2048]{2,0,1:T(8,128)(2,1)}) %all-gather.2.cloned.1.call-update) | async-done | bytes 12582928 | tf_op jit(solution)/shard_map/all_gather | solution.py:152
  184.8 8.6 %fusion.6 = f32[3072,1,384]{0,2,1:T(8,128)S(1)} fusion(bf16[2048,384]{0,1:T(8,128)(2,1)} %bitcast.106, bf16[3072,1,2048]{2,0,1:T(8,128)(2,1)} %all-gather.2.cloned.1.call-done), kind=kOutput, calls=%fused_computation.13 | convolution fusion | flops 4831838208 | bytes 18874368 | tf_op jit(solution)/shard_map/red,edk->rek/dot_general | solution.py:150
  193.4 6.5 %convert_bitcast_fusion = bf16[3072,1,2048]{2,0,1:T(8,128)(2,1)} fusion(f32[3072,1,384]{0,2,1:T(8,128)S(1)} %fusion.6, bf16[1,192,2048]{2,1,0:T(8,128)(2,1)S(1)} %copy-done.12), kind=kOutput, calls=%fused_computation.7 | convolution fusion | flops 2425749504 | bytes 18087936 | tf_op jit(solution)/shard_map/ref,efd->red/dot_general | solution.py:157
  199.9 114.9 %reduce-scatter.3.cloned.1.call-done = bf16[768,1,2048]{2,0,1:T(8,128)(2,1)} async-done(((bf16[3072,1,2048]{2,0,1:T(8,128)(2,1)}), bf16[768,1,2048]{2,0,1:T(8,128)(2,1)}) %reduce-scatter.3.cloned.1.call-update) | async-done | bytes 3145744 | tf_op jit(solution)/shard_map/reduce_scatter | solution.py:23
  315.6 1.3 gather_fusion.1
  317.2 43.9 %reduce-scatter.5.cloned.1.call-done = bf16[96,1,2048]{2,0,1:T(8,128)(2,1)} async-done(((bf16[768,1,2048]{2,0,1:T(8,128)(2,1)}), bf16[96,1,2048]{2,0,1:T(8,128)(2,1)}) %reduce-scatter.5.cloned.1.call-update) | async-done | bytes 393232 | tf_op jit(solution)/shard_map/reduce_scatter | solution.py:23
  361.1 1.9 reshape.337
  363.0 8.1 %all-to-all-start.1 = ((bf16[8,12,2048]{2,1,0:T(8,128)(2,1)}), bf16[8,12,2048]{2,1,0:T(8,128)(2,1)S(1)}, u32[]{:S(2)}, u32[]{:S(2)}) async-start(bf16[8,12,2048]{2,1,0:T(8,128)(2,1)} %reshape.337), calls=%async_computation.3 | async-start | bytes 1048576 | tf_op jit(solution)/shard_map/all_to_all | solution.py:165
  371.7 8.8 %all-to-all-done.1 = bf16[8,12,2048]{2,1,0:T(8,128)(2,1)S(1)} async-done(((bf16[8,12,2048]{2,1,0:T(8,128)(2,1)}), bf16[8,12,2048]{2,1,0:T(8,128)(2,1)S(1)}, u32[]{:S(2)}, u32[]{:S(2)}) %all-to-all-start.1) | async-done | bytes 393248 | tf_op jit(solution)/shard_map/all_to_all | solution.py:165
  380.6 0.8 gather_fusion
  381.8 0.9 multiply_reduce_fusion
  382.8 3.2 convolution_convert_fusion.7
  386.8 2.1 fusion.19
  (104 shorter events, 9.5 us)
Async XLA Ops:
  7.2 44.3 %copy-start = (bf16[512,2048]{1,0:T(8,128)(2,1)S(1)}, bf16[512,2048]{1,0:T(8,128)(2,1)}, u32[]{:S(2)}) copy-start(bf16[512,2048]{1,0:T(8,128)(2,1)} %param.25) | copy-start | bytes 6291460
  7.2 13.7 %copy-start.11 = (s32[256]{0:T(256)S(1)}, s32[256]{0:T(256)}, u32[]{:S(2)}) copy-start(s32[256]{0:T(256)} %param.18) | copy-start | bytes 3076
  7.2 14.9 %copy-start.10 = (s32[40,2]{0,1:T(2,128)S(1)}, s32[40,2]{0,1:T(2,128)}, u32[]{:S(2)}) copy-start(s32[40,2]{0,1:T(2,128)} %param.19) | copy-start | bytes 964
  7.2 177.6 %all-gather.2.cloned.1.call-start = ((), (), s32[]{:S(2)}) async-start(), calls=%async_computation.4 | async-start | bytes 12976128 | tf_op jit(solution)/shard_map/all_gather | solution.py:152
  10.3 17.0 %collective-permute-start.1 = (bf16[256,512]{1,0:T(8,128)(2,1)}, bf16[256,512]{1,0:T(8,128)(2,1)}, u32[]{:S(2)}, u32[]{:S(2)}) collective-permute-start(bf16[256,512]{1,0:T(8,128)(2,1)} %fusion.34), channel_id=1, source_target_pairs={{0,1},{1,2},{2,3},{3,4},{4,5},{5,6},{6,7},{7,8},{8,9},{9,10},{10,1... | collective-permute-start | bytes 786440 | tf_op jit(solution)/shard_map/ppermute | solution.py:30
  14.8 14.2 %collective-permute-start = (bf16[256,512]{1,0:T(8,128)(2,1)}, bf16[256,512]{1,0:T(8,128)(2,1)}, u32[]{:S(2)}, u32[]{:S(2)}) collective-permute-start(bf16[256,512]{1,0:T(8,128)(2,1)} %fusion.34), channel_id=1, source_target_pairs={{0,2},{1,3},{2,4},{3,5},{4,6},{5,7},{6,8},{7,9},{8,10},{9,11},{10,... | collective-permute-start | bytes 786440 | tf_op jit(solution)/shard_map/ppermute | solution.py:30
  30.9 4.5 %copy-start.6 = (bf16[256,512]{0,1:T(8,128)(2,1)S(1)}, bf16[256,512]{0,1:T(8,128)(2,1)}, u32[]{:S(2)}) copy-start(bf16[256,512]{0,1:T(8,128)(2,1)} %copy.79) | copy-start | bytes 786436
  30.9 4.5 %copy-start.7 = (pred[256,768]{1,0:T(8,128)(4,1)S(1)}, pred[256,768]{1,0:T(8,128)(4,1)}, u32[]{:S(2)}) copy-start(pred[256,768]{1,0:T(8,128)(4,1)} %compare_and_fusion) | copy-start | bytes 589828
  35.4 6.2 %copy-start.3 = (bf16[768,512]{0,1:T(8,128)(2,1)S(1)}, bf16[768,512]{0,1:T(8,128)(2,1)}, u32[]{:S(2)}) copy-start(bf16[768,512]{0,1:T(8,128)(2,1)} %copy.81) | copy-start | bytes 2359300
  41.6 4.1 %copy-start.2 = (bf16[256,512]{1,0:T(8,128)(2,1)S(1)}, bf16[256,512]{1,0:T(8,128)(2,1)}, u32[]{:S(2)}) copy-start(bf16[256,512]{1,0:T(8,128)(2,1)} %param.17) | copy-start | bytes 786436
  41.6 4.1 %copy-start.13 = (bf16[512,512]{1,0:T(8,128)(2,1)S(1)}, bf16[512,512]{1,0:T(8,128)(2,1)}, u32[]{:S(2)}) copy-start(bf16[512,512]{1,0:T(8,128)(2,1)} %param.22) | copy-start | bytes 1572868
  41.6 6.3 %copy-start.5 = (bf16[512,512]{1,0:T(8,128)(2,1)S(1)}, bf16[512,512]{1,0:T(8,128)(2,1)}, u32[]{:S(2)}) copy-start(bf16[512,512]{1,0:T(8,128)(2,1)} %param.23) | copy-start | bytes 1572868
  50.1 2.0 copy-start.9
  66.2 248.6 %reduce-scatter.3.cloned.1.call-start = ((), (), s32[]{:S(2)}) async-start(), calls=%async_computation.5 | async-start | bytes 15728640 | tf_op jit(solution)/shard_map/reduce_scatter | solution.py:23
  184.8 8.6 %copy-start.12 = (bf16[1,192,2048]{2,1,0:T(8,128)(2,1)S(1)}, bf16[1,192,2048]{2,1,0:T(8,128)(2,1)}, u32[]{:S(2)}) copy-start(bf16[1,192,2048]{2,1,0:T(8,128)(2,1)} %param.29) | copy-start | bytes 2359300
  199.9 115.4 %copy-start.8 = (f32[2048,8]{0,1:T(8,128)S(1)}, f32[2048,8]{0,1:T(8,128)}, u32[]{:S(2)}) copy-start(f32[2048,8]{0,1:T(8,128)} %param.27) | copy-start | bytes 196612
  199.9 161.2 %reduce-scatter.5.cloned.1.call-start = ((), (), s32[]{:S(2)}) async-start(), calls=%async_computation.6 | async-start | bytes 3538944 | tf_op jit(solution)/shard_map/reduce_scatter | solution.py:23
  315.6 55.6 %copy-start.14 = (bf16[512,512]{1,0:T(8,128)(2,1)S(1)}, bf16[512,512]{1,0:T(8,128)(2,1)}, u32[]{:S(2)}) copy-start(bf16[512,512]{1,0:T(8,128)(2,1)} %param.31) | copy-start | bytes 1572868
  315.6 55.6 %copy-start.15 = (f32[512]{0:T(512)S(1)}, f32[512]{0:T(512)}, u32[]{:S(2)}) copy-start(f32[512]{0:T(512)} %param.30) | copy-start | bytes 6148
  363.0 17.5 %all-to-all-start.1 = ((bf16[8,12,2048]{2,1,0:T(8,128)(2,1)}), bf16[8,12,2048]{2,1,0:T(8,128)(2,1)S(1)}, u32[]{:S(2)}, u32[]{:S(2)}) async-start(bf16[8,12,2048]{2,1,0:T(8,128)(2,1)} %reshape.337), calls=%async_computation.3 | async-start | bytes 1048576 | tf_op jit(solution)/shard_map/all_to_all | solution.py:165
  382.7 4.0 %copy-start.4 = (bf16[40,2048]{1,0:T(8,128)(2,1)}, bf16[40,2048]{1,0:T(8,128)(2,1)S(1)}, u32[]{:S(2)}) copy-start(bf16[40,2048]{1,0:T(8,128)(2,1)S(1)} %add_convert_fusion) | copy-start | bytes 491524
  382.8 6.1 %copy-start.1 = (bf16[512,2048]{1,0:T(8,128)(2,1)S(1)}, bf16[512,2048]{1,0:T(8,128)(2,1)}, u32[]{:S(2)}) copy-start(bf16[512,2048]{1,0:T(8,128)(2,1)} %param.25) | copy-start | bytes 6291460
Sparse Core Ops, SparseCore 0:
  66.4 118.3 all-gather.1
  200.0 114.7 reduce-scatter.2
  317.4 43.6 reduce-scatter.4
where the time goes:
time: 396 us; the launch traced here: 395 us
  waiting for transfers between devices  286 us (72%)
  matrix products  41.2 us (10%)
  starting transfers between devices  16.9 us (4%)
  local copies, waits for them, and re-layouts  14.8 us (4%)
  between operations  14.2 us (4%)
  blocking collectives  12.9 us (3%)
  other arithmetic  9.47 us (2%)
    reduce_scatter x2, waiting for transfers between devices, own_rows(): subtotal = lax.psum_scatter(subtotal, axis, scatter_dimension=0, tiled=True)  159 us
    all_gather x1, waiting for transfers between devices, mixture(): lax.all_gather(rows, SEQ, axis=0, tiled=True)  118 us
    all_to_all x1, blocking collectives, mixture(): lax.all_to_all(routed.reshape(expert_devices, capacity * local_experts, g...  12.9 us
    all_to_all x1, waiting for transfers between devices, mixture(): lax.all_to_all(results, 'expert', split_axis=0, concat_axis=0, tiled=True)  8.75 us
    dot_general x1, matrix products, mixture(): jnp.einsum('red,edk->rek', lax.all_gather(rows, SEQ, axis=0, tiled=True),...  8.58 us
    ppermute x2, starting transfers between devices, passed_along(): return lax.ppermute(x, axis, pairs)  8.48 us
    all_to_all x1, starting transfers between devices, mixture(): lax.all_to_all(results, 'expert', split_axis=0, concat_axis=0, tiled=True)  8.13 us
  transfers between devices with their start and end apart: 6, of which 4 were waited for; matrix products, arithmetic and copies ran while one was open for 3% of the time, Pallas kernels for 0%

commit v1 on v0

--- a/solution.py
+++ b/solution.py
@@ -15,13 +15,6 @@
 
 epsilon = 1e-06
 very_negative = -1e30
-
-
-def own_rows(terms, axes):
-    subtotal = terms.astype(jnp.bfloat16)
-    for axis in axes:
-        subtotal = lax.psum_scatter(subtotal, axis, scatter_dimension=0, tiled=True)
-    return subtotal.astype(jnp.float32)
 
 
 def passed_along(x, axis, by):
@@ -89,9 +82,10 @@
         heads_split(pairs[:, width_local:]),
         member,
     )
-    patch_input = (pooled.astype(jnp.float32) + mixed).astype(jnp.bfloat16)
-    state = jnp.dot(patch_input, w_up, preferred_element_type=jnp.float32)
-    return jnp.where(live[:, None], state, jnp.zeros_like(state)).astype(jnp.bfloat16)
+    summed = pooled.astype(jnp.float32) + mixed
+    patch_input = jnp.where(live[:, None], summed, 0.0).astype(jnp.bfloat16)
+    state = jnp.dot(patch_input, w_up, preferred_element_type=jnp.float32).astype(jnp.bfloat16)
+    return patch_input, state
 
 
 def decode_block(encoded, flags, states, dec_gain, w_dq, w_dkv, w_do):
@@ -120,52 +114,60 @@
     return jnp.sum(ranked * onehot, axis=1).reshape(expert_ids.shape)
 
 
-def mixture(patch_state, expert_ids, moe_gain, w_router, w_in, w_down):
+def folded_weights(w_up, moe_gain, w_in, w_down):
+    scaled = (w_up.astype(jnp.float32) * moe_gain).astype(jnp.bfloat16)
+    gate = lax.dot_general(w_in[0, :, 0, :], scaled, (((0,), (1,)), ((), ())), preferred_element_type=jnp.float32)
+    upper = lax.dot_general(w_in[0, :, 1, :], scaled, (((0,), (1,)), ((), ())), preferred_element_type=jnp.float32)
+    return jnp.concatenate(
+        [gate.astype(jnp.bfloat16), upper.astype(jnp.bfloat16), w_down[0]], axis=1
+    )
+
+
+def mixture(patch_input, patch_state, expert_ids, moe_gain, w_router, weights):
+    width = patch_input.shape[1]
     patch_cap = patch_state.shape[0]
-    global_width = patch_state.shape[1]
     experts = w_router.shape[1]
-    local_experts = w_in.shape[0]
-    expert_devices = experts // local_experts
     capacity = 12 * patch_cap // (5 * experts)
-    hidden_share = w_in.shape[3]
-    normed = rms_scale(patch_state, moe_gain).astype(jnp.bfloat16)
+    widened = patch_state.astype(jnp.float32)
+    scale = lax.rsqrt(jnp.mean(widened * widened, axis=-1, keepdims=True) + epsilon)
+    normed = (widened * scale * moe_gain).astype(jnp.bfloat16)
     logits = jnp.dot(normed.astype(jnp.float32), w_router, precision=lax.Precision.HIGHEST)
-    gates = softmax_rows(jnp.take_along_axis(logits, expert_ids, axis=1))
+    picked = expert_ids[:, :, None] == jnp.arange(experts, dtype=jnp.int32)[None, None, :]
+    gates = softmax_rows(jnp.sum(jnp.where(picked, logits[:, None, :], 0.0), axis=2))
     slot_number = route_slots(expert_ids, experts)
-    target = (
-        expert_ids // local_experts * capacity + slot_number
-    ) * local_experts + expert_ids % local_experts
+    target = expert_ids * capacity + slot_number
     places = jnp.arange(experts * capacity, dtype=jnp.int32)
-    dispatch = jnp.sum((target[None, :, :] == places[:, None, None]).astype(jnp.bfloat16), axis=2)
-    routed = jnp.dot(dispatch, normed, preferred_element_type=jnp.float32).astype(jnp.bfloat16)
+    chosen = target[None, :, :] == places[:, None, None]
+    dispatch = jnp.sum(chosen.astype(jnp.bfloat16), axis=2)
+    sent = (patch_input.astype(jnp.float32) * scale).astype(jnp.bfloat16)
+    routed = jnp.dot(dispatch, sent, preferred_element_type=jnp.float32).astype(jnp.bfloat16)
     arrived = lax.all_to_all(
-        routed.reshape(expert_devices, capacity * local_experts, global_width),
-        "expert",
-        split_axis=0,
-        concat_axis=0,
-        tiled=True,
-    )
-    rows = arrived.reshape(expert_devices * capacity, local_experts, global_width)
-    paired = w_in.reshape(local_experts, global_width, 2 * hidden_share)
-    both = jnp.einsum(
-        "red,edk->rek",
-        lax.all_gather(rows, SEQ, axis=0, tiled=True),
-        paired,
-        preferred_element_type=jnp.float32,
-    )
-    hidden = (jax.nn.silu(both[..., :hidden_share]) * both[..., hidden_share:]).astype(jnp.bfloat16)
-    term = jnp.einsum("ref,efd->red", hidden, w_down, preferred_element_type=jnp.float32).astype(
+        routed.reshape(experts, capacity, width), "expert", split_axis=0, concat_axis=0, tiled=True
+    )
+    rows = lax.all_gather(
+        arrived.reshape(experts * capacity, width), "seq_1", axis=0, tiled=True
+    )
+    over = (((1,), (1,)), ((), ()))
+    gate = lax.dot_general(rows, weights[:, :width], over, preferred_element_type=jnp.float32)
+    upper = lax.dot_general(
+        rows, weights[:, width : 2 * width], over, preferred_element_type=jnp.float32
+    )
+    hidden = (jax.nn.silu(gate) * upper).astype(jnp.bfloat16)
+    term = jnp.dot(hidden, weights[:, 2 * width :], preferred_element_type=jnp.float32).astype(
         jnp.bfloat16
     )
-    term = lax.optimization_barrier(term)
-    summed = own_rows(term.astype(jnp.float32), SEQ)
-    results = summed.astype(jnp.bfloat16).reshape(
-        expert_devices, capacity * local_experts, global_width
-    )
-    returned = lax.all_to_all(results, "expert", split_axis=0, concat_axis=0, tiled=True)
-    chosen = returned.reshape(experts * capacity, global_width)[target]
-    combined = jnp.sum(gates[..., None] * chosen.astype(jnp.float32), axis=1)
-    return (patch_state.astype(jnp.float32) + combined).astype(jnp.bfloat16)
+    summed = lax.psum_scatter(term, "seq_1", scatter_dimension=0, tiled=True)
+    returned = lax.all_to_all(
+        summed.reshape(experts, capacity, -1), "expert", split_axis=0, concat_axis=0, tiled=True
+    ).reshape(experts * capacity, -1)
+    weighted = jnp.sum(jnp.where(chosen, gates[None], 0.0), axis=2)
+    high = weighted.astype(jnp.bfloat16)
+    low = (weighted - high.astype(jnp.float32)).astype(jnp.bfloat16)
+    rows_over = (((0,), (0,)), ((), ()))
+    combined = lax.dot_general(
+        high, returned, rows_over, preferred_element_type=jnp.float32
+    ) + lax.dot_general(low, returned, rows_over, preferred_element_type=jnp.float32)
+    return (widened + combined).astype(jnp.bfloat16)
 
 
 def per_device(
@@ -187,6 +189,9 @@
     w_dkv,
     w_do,
 ):
+    weights = lax.all_gather(
+        folded_weights(w_up, moe_gain, w_in, w_down), "seq_0", axis=0, tiled=True
+    )
     byte_dev = byte_states.shape[0]
     model_width = byte_states.shape[1]
     normed = rms_scale(byte_states, enc_gain).astype(jnp.bfloat16)
@@ -215,8 +220,8 @@
     encoded = (
         byte_states.astype(jnp.float32) + jnp.dot(mixed, w_out, preferred_element_type=jnp.float32)
     ).astype(jnp.bfloat16)
-    patch_state = patch_block(encoded, patch_start, w_xq, w_xkv, w_up)
-    patch_out = mixture(patch_state, expert_ids, moe_gain, w_router, w_in, w_down)
+    patch_input, patch_state = patch_block(encoded, patch_start, w_xq, w_xkv, w_up)
+    patch_out = mixture(patch_input, patch_state, expert_ids, moe_gain, w_router, weights)
     bytes_out = decode_block(encoded, patch_start, patch_out, dec_gain, w_dq, w_dkv, w_do)
     return (bytes_out, patch_out)
 

time: 396 us -> 174 us (0.44)
  waiting for transfers between devices: 286 us -> 53.2 us
  blocking collectives: 12.9 us -> 33.9 us
  local copies, waits for them, and re-layouts: 14.8 us -> 8.06 us
    all_gather x1, waiting for transfers between devices: 118 us -> 0.01 us  [per_device(): lax.all_gather(folded_weights(w_up, moe_gain, w_in, w_down), 'seq_0', axi...]
    reduce_scatter x2 -> x1, waiting for transfers between devices: 159 us -> 44.1 us  [mixture(): summed = lax.psum_scatter(term, 'seq_1', scatter_dimension=0, tiled=True)]
    all_gather x0 -> x1, blocking collectives: none -> 25 us  [mixture(): lax.all_gather(arrived.reshape(experts * capacity, width), 'seq_1', axis=...]
    all_to_all x1, blocking collectives: 12.9 us -> 8.88 us  [mixture(): lax.all_to_all(routed.reshape(experts, capacity, width), 'expert', split_...]
    dot_general x4 -> x8, matrix products: 16 us -> 17.5 us  [the longest x1 7.78 us: mixture(): jnp.dot(hidden, weights[:, 2 * width:], preferred_element_type=jnp.float32)]
  transfers between devices with their start and end apart: 6 -> 5, of which waited for: 4 -> 2; matrix products, arithmetic and copies ran while one was open for 3% -> 19% of each run, Pallas kernels for 0% -> 0%
where the time goes in v1:
time: 174 us
  waiting for transfers between devices  53.2 us (31%)
  matrix products  37.9 us (22%)
  blocking collectives  33.9 us (19%)
  starting transfers between devices  16.8 us (10%)
  between operations  14.6 us (8%)
  other arithmetic  9.06 us (5%)
  local copies, waits for them, and re-layouts  8.06 us (5%)
    reduce_scatter x1, waiting for transfers between devices, mixture(): summed = lax.psum_scatter(term, 'seq_1', scatter_dimension=0, tiled=True)  44.1 us
    all_gather x1, blocking collectives, mixture(): lax.all_gather(arrived.reshape(experts * capacity, width), 'seq_1', axis=...  25 us
    all_to_all x1, waiting for transfers between devices, mixture(): lax.all_to_all(summed.reshape(experts, capacity, -1), 'expert', split_axi...  9.08 us
    all_to_all x1, blocking collectives, mixture(): lax.all_to_all(routed.reshape(experts, capacity, width), 'expert', split_...  8.88 us
    ppermute x2, starting transfers between devices, passed_along(): return lax.ppermute(x, axis, pairs)  8.76 us
    all_to_all x1, starting transfers between devices, mixture(): lax.all_to_all(summed.reshape(experts, capacity, -1), 'expert', split_axi...  7.96 us
    dot_general x1, matrix products, mixture(): jnp.dot(hidden, weights[:, 2 * width:], preferred_element_type=jnp.float32)  7.78 us
    sub x1, matrix products, softmax_rows(): raised = jnp.exp(scores - highest)  5.99 us
  transfers between devices with their start and end apart: 5, of which 2 were waited for; matrix products, arithmetic and copies ran while one was open for 19% of the time, Pallas kernels for 0%

profile of v1, /device:TPU:1, one launch (start us, length us, event | category | flops | bytes accessed | tf_op | source)
XLA Modules:
  0.0 173.6 jit_solution(16134973871708597751)
XLA Ops:
  7.2 1.2 fusion.40
  8.4 1.1 fusion.42
  9.5 4.8 %collective-permute-start.1 = (bf16[256,512]{1,0:T(8,128)(2,1)S(1)}, bf16[256,512]{1,0:T(8,128)(2,1)}, u32[]{:S(2)}, u32[]{:S(2)}) collective-permute-start(bf16[256,512]{1,0:T(8,128)(2,1)S(1)} %fusion.42), channel_id=1, source_target_pairs={{0,1},{1,2},{2,3},{3,4},{4,5},{5,6},{6,7},{7,8},{8,9},{9,10},{10,1... | collective-permute-start | bytes 786440 | tf_op jit(solution)/shard_map/ppermute | solution.py:23
  14.4 3.9 %collective-permute-start = (bf16[256,512]{1,0:T(8,128)(2,1)S(1)}, bf16[256,512]{1,0:T(8,128)(2,1)}, u32[]{:S(2)}, u32[]{:S(2)}) collective-permute-start(bf16[256,512]{1,0:T(8,128)(2,1)S(1)} %fusion.42), channel_id=1, source_target_pairs={{0,2},{1,3},{2,4},{3,5},{4,6},{5,7},{6,8},{7,9},{8,10},{9,11},{10,... | collective-permute-start | bytes 786440 | tf_op jit(solution)/shard_map/ppermute | solution.py:23
  18.3 2.6 %fusion.26 = bf16[192,512]{1,0:T(8,128)(2,1)S(1)} fusion(bf16[512,2048]{1,0:T(8,128)(2,1)} %param.25, f32[2048]{0:T(1024)} %param.26, bf16[1,2048,2,192]{1,3,2,0:T(8,128)(2,1)} %param.28), kind=kOutput, calls=%fused_computation.47 | convolution fusion | flops 405897216 | bytes 3088384 | tf_op jit(solution)/shard_map/dot_general | solution.py:120
  21.0 0.9 fusion.27
  22.1 1.1 pad_maximum_fusion.1
  23.3 0.6 reduce_sum.114
  25.5 0.6 convolution_convert_fusion.1
  26.1 0.7 iota_compare_fusion.5
  26.8 0.7 slice.66
  27.5 1.8 %copy.62 = bf16[256,512]{0,1:T(8,128)(2,1)} copy(bf16[256,512]{1,0:T(8,128)(2,1)} %slice.66) | data formatting | bytes 524288 | tf_op jit(solution)/shard_map/slice | solution.py:199
  29.3 1.0 compare_and_fusion
  30.3 1.4 convolution_convert_fusion.4
  31.7 1.4 convolution_convert_fusion.5
  33.9 6.0 %fusion.78 = (f32[8,256]{1,0:T(8,128)S(1)}, f32[8,256,768]{2,1,0:T(8,128)}) fusion(pred[256,768]{1,0:T(8,128)(4,1)} %compare_and_fusion, bf16[8,256,64]{1,2,0:T(8,128)(2,1)} %bitcast.89, bf16[8,768,64]{1,2,0:T(8,128)(2,1)S(1)} %bitcast.85), kind=kOutput, calls=%fused_computation.133 | convolution fusion | flops 207618816 | bytes 7544832 | tf_op jit(solution)/shard_map/sub | solution.py:37
  39.9 4.0 %fusion.18 = bf16[8,256,64]{1,2,0:T(8,128)(2,1)S(1)} fusion(bf16[8,768,64]{1,2,0:T(8,128)(2,1)S(1)} %bitcast.86, f32[8,256,768]{2,1,0:T(8,128)} %get-tuple-element.9, f32[8,256]{1,0:T(8,128)S(1)} %get-tuple-element.8), kind=kOutput, calls=%fused_computation.36 | convolution fusion | flops 204603392 | bytes 7348224 | tf_op jit(solution)/shard_map/hqk,hkd->hqd/dot_general | solution.py:55
  44.3 1.8 %select_reduce_fusion = bf16[40,512]{1,0:T(8,128)(2,1)S(1)} fusion(pred[40,256]{1,0:T(8,128)(4,1)S(1)} %iota_compare_fusion.2, bf16[256,512]{1,0:T(8,128)(2,1)S(1)} %get-tuple-element.11), kind=kLoop, calls=%fused_computation.3 | loop fusion | flops 10465280 | bytes 313344 | tf_op jit(solution)/shard_map/reduce_max | solution.py:71
  46.6 0.4 convolution_convert_fusion.3
  47.7 0.6 convolution_bitcast_fusion
  48.6 2.2 %multiply_reduce_fusion = (f32[40]{0:T(128)S(1)}, f32[40,2048]{1,0:T(8,128)S(1)}) fusion(bf16[40,512]{1,0:T(8,128)(2,1)S(1)} %select_convert_fusion, bf16[512,2048]{1,0:T(8,128)(2,1)} %param.25), kind=kOutput, calls=%fused_computation.76 | convolution fusion | flops 84213720 | bytes 2465952 | tf_op jit(solution)/shard_map/dot_general | solution.py:87
  51.1 8.9 %all_to_all.10 = bf16[8,12,512]{2,1,0:T(8,128)(2,1)S(1)} all-to-all(bf16[8,12,512]{2,1,0:T(8,128)(2,1)S(1)} %reshape.313), channel_id=1, replica_groups=mesh['seq_0'=4,'seq_1'=8,'expert'=8] {'expert'}, dimensions={0} | all-to-all | bytes 196608 | tf_op jit(solution)/shard_map/all_to_all | solution.py:144
  60.0 25.0 %all_gather.6 = bf16[768,512]{1,0:T(8,128)(2,1)S(1)} all-gather(bf16[96,512]{1,0:T(8,128)(2,1)S(1)} %reshape.314), channel_id=1, replica_groups=mesh['seq_0'=4,'seq_1'=8,'expert'=8] {'seq_1'}, dimensions={0}, use_global_device_ids=true | all-gather | bytes 884736 | tf_op jit(solution)/shard_map/all_gather | solution.py:147
  85.0 3.4 %fusion.32 = f32[768,768]{1,0:T(8,128)} fusion(bf16[768,512]{1,0:T(8,128)(2,1)S(1)} %all_gather.6, bf16[768,3072]{1,0:T(8,128)(2,1)} %all-gather.2.cloned.1.call-done), kind=kOutput, calls=%fused_computation.56 | convolution fusion | flops 603979776 | bytes 3932160 | tf_op jit(solution)/shard_map/dot_general | solution.py:151
  88.4 7.8 %convolution_convert_fusion = bf16[768,2048]{1,0:T(8,128)(2,1)} fusion(bf16[768,3072]{1,0:T(8,128)(2,1)} %all-gather.2.cloned.1.call-done, f32[768,768]{1,0:T(8,128)} %fusion.32, bf16[768,512]{1,0:T(8,128)(2,1)S(1)} %all_gather.6), kind=kOutput, calls=%fused_computation.9 | convolution fusion | flops 3025010688 | bytes 10223616 | tf_op jit(solution)/shard_map/dot_general | solution.py:156
  96.2 0.8 copy-done.8
  97.8 44.1 %reduce-scatter.2.cloned.1.call-done = bf16[96,2048]{1,0:T(8,128)(2,1)} async-done(((bf16[768,2048]{1,0:T(8,128)(2,1)}), bf16[96,2048]{1,0:T(8,128)(2,1)}) %reduce-scatter.2.cloned.1.call-update) | async-done | bytes 393232 | tf_op jit(solution)/shard_map/reduce_scatter | solution.py:159
  141.9 1.9 %reshape.315 = bf16[8,12,2048]{2,1,0:T(8,128)(2,1)} reshape(bf16[96,2048]{1,0:T(8,128)(2,1)} %reduce-scatter.2.cloned.1.call-done) | data formatting | bytes 786432 | tf_op jit(solution)/shard_map/reshape | solution.py:161
  143.7 8.0 %all-to-all-start.1 = ((bf16[8,12,2048]{2,1,0:T(8,128)(2,1)}), bf16[8,12,2048]{2,1,0:T(8,128)(2,1)S(1)}, u32[]{:S(2)}, u32[]{:S(2)}) async-start(bf16[8,12,2048]{2,1,0:T(8,128)(2,1)} %reshape.315), calls=%async_computation.2 | async-start | bytes 1048576 | tf_op jit(solution)/shard_map/all_to_all | solution.py:160
  152.0 9.1 %all-to-all-done.1 = bf16[8,12,2048]{2,1,0:T(8,128)(2,1)S(1)} async-done(((bf16[8,12,2048]{2,1,0:T(8,128)(2,1)}), bf16[8,12,2048]{2,1,0:T(8,128)(2,1)S(1)}, u32[]{:S(2)}, u32[]{:S(2)}) %all-to-all-start.1) | async-done | bytes 393248 | tf_op jit(solution)/shard_map/all_to_all | solution.py:160
  161.6 3.1 %convolution_convert_fusion.9 = bf16[40,1024]{1,0:T(8,128)(2,1)S(1)} fusion(bf16[40,2048]{1,0:T(8,128)(2,1)S(1)} %fusion.10, bf16[2048,1024]{1,0:T(8,128)(2,1)} %param.32), kind=kOutput, calls=%fused_computation.51 | convolution fusion | flops 167813120 | bytes 4440064 | tf_op jit(solution)/shard_map/dot_general | solution.py:96
  165.7 1.0 fusion.17
  (96 shorter events, 7.1 us)
Async XLA Ops:
  7.2 39.4 %copy-start = (bf16[512,1024]{1,0:T(8,128)(2,1)S(1)}, bf16[512,1024]{1,0:T(8,128)(2,1)}, u32[]{:S(2)}) copy-start(bf16[512,1024]{1,0:T(8,128)(2,1)} %param.24) | copy-start | bytes 3145732
  7.2 77.8 %all-gather.2.cloned.1.call-start = ((), (), s32[]{:S(2)}) async-start(), calls=%async_computation.3 | async-start | bytes 5898240 | tf_op jit(solution)/shard_map/all_gather | solution.py:192
  9.5 11.4 %copy-start.1 = (bf16[512,2048]{1,0:T(8,128)(2,1)S(1)}, bf16[512,2048]{1,0:T(8,128)(2,1)}, u32[]{:S(2)}) copy-start(bf16[512,2048]{1,0:T(8,128)(2,1)} %param.25) | copy-start | bytes 6291460
  9.5 11.4 %copy-start.10 = (f32[2048]{0:T(1024)S(1)}, f32[2048]{0:T(1024)}, u32[]{:S(2)}) copy-start(f32[2048]{0:T(1024)} %param.26) | copy-start | bytes 24580
  9.5 11.4 %copy-start.12 = (bf16[1,2048,2,192]{1,3,2,0:T(8,128)(2,1)S(1)}, bf16[1,2048,2,192]{1,3,2,0:T(8,128)(2,1)}, u32[]{:S(2)}) copy-start(bf16[1,2048,2,192]{1,3,2,0:T(8,128)(2,1)} %param.28) | copy-start | bytes 4718596
  9.5 20.7 %collective-permute-start.1 = (bf16[256,512]{1,0:T(8,128)(2,1)S(1)}, bf16[256,512]{1,0:T(8,128)(2,1)}, u32[]{:S(2)}, u32[]{:S(2)}) collective-permute-start(bf16[256,512]{1,0:T(8,128)(2,1)S(1)} %fusion.42), channel_id=1, source_target_pairs={{0,1},{1,2},{2,3},{3,4},{4,5},{5,6},{6,7},{7,8},{8,9},{9,10},{10,1... | collective-permute-start | bytes 786440 | tf_op jit(solution)/shard_map/ppermute | solution.py:23
  14.4 17.3 %collective-permute-start = (bf16[256,512]{1,0:T(8,128)(2,1)S(1)}, bf16[256,512]{1,0:T(8,128)(2,1)}, u32[]{:S(2)}, u32[]{:S(2)}) collective-permute-start(bf16[256,512]{1,0:T(8,128)(2,1)S(1)} %fusion.42), channel_id=1, source_target_pairs={{0,2},{1,3},{2,4},{3,5},{4,6},{5,7},{6,8},{7,9},{8,10},{9,11},{10,... | collective-permute-start | bytes 786440 | tf_op jit(solution)/shard_map/ppermute | solution.py:23
  21.0 1.1 copy-start.4
  21.9 1.5 copy-start.11
  21.9 2.6 %copy-start.9 = (s32[40,2]{0,1:T(2,128)S(1)}, s32[40,2]{0,1:T(2,128)}, u32[]{:S(2)}) copy-start(s32[40,2]{0,1:T(2,128)} %param.19) | copy-start | bytes 964
  21.9 3.6 %copy-start.2 = (bf16[512,1536]{1,0:T(8,128)(2,1)S(1)}, bf16[512,1536]{1,0:T(8,128)(2,1)}, u32[]{:S(2)}) copy-start(bf16[512,1536]{1,0:T(8,128)(2,1)} %param.21) | copy-start | bytes 4718596
  23.2 118.6 %reduce-scatter.2.cloned.1.call-start = ((), (), s32[]{:S(2)}) async-start(), calls=%async_computation.4 | async-start | bytes 3538944 | tf_op jit(solution)/shard_map/reduce_scatter | solution.py:159
  39.9 4.0 %copy-start.3 = (bf16[256,512]{1,0:T(8,128)(2,1)S(1)}, bf16[256,512]{1,0:T(8,128)(2,1)}, u32[]{:S(2)}) copy-start(bf16[256,512]{1,0:T(8,128)(2,1)} %param.17) | copy-start | bytes 786436
  39.9 4.1 %copy-start.13 = (bf16[512,512]{1,0:T(8,128)(2,1)S(1)}, bf16[512,512]{1,0:T(8,128)(2,1)}, u32[]{:S(2)}) copy-start(bf16[512,512]{1,0:T(8,128)(2,1)} %param.22) | copy-start | bytes 1572868
  39.9 6.3 %copy-start.6 = (bf16[512,512]{1,0:T(8,128)(2,1)S(1)}, bf16[512,512]{1,0:T(8,128)(2,1)}, u32[]{:S(2)}) copy-start(bf16[512,512]{1,0:T(8,128)(2,1)} %param.23) | copy-start | bytes 1572868
  96.2 0.8 copy-start.8
  96.2 1.2 copy-start.14
  96.2 1.2 copy-start.15
  143.7 17.3 %all-to-all-start.1 = ((bf16[8,12,2048]{2,1,0:T(8,128)(2,1)}), bf16[8,12,2048]{2,1,0:T(8,128)(2,1)S(1)}, u32[]{:S(2)}, u32[]{:S(2)}) async-start(bf16[8,12,2048]{2,1,0:T(8,128)(2,1)} %reshape.315), calls=%async_computation.2 | async-start | bytes 1048576 | tf_op jit(solution)/shard_map/all_to_all | solution.py:160
  161.5 3.2 %copy-start.5 = (bf16[40,2048]{1,0:T(8,128)(2,1)}, bf16[40,2048]{1,0:T(8,128)(2,1)S(1)}, u32[]{:S(2)}) copy-start(bf16[40,2048]{1,0:T(8,128)(2,1)S(1)} %fusion.10) | copy-start | bytes 491524
  164.6 1.0 copy-start.7
Sparse Core Ops, SparseCore 0:
  23.4 55.5 all-gather.1
  96.3 45.4 reduce-scatter.1

commit v2 on v1

--- a/solution.py
+++ b/solution.py
@@ -1,8 +1,11 @@
+import functools
 import math
 
 import jax
 import jax.numpy as jnp
 from jax import lax
+from jax.experimental import pallas as pl
+from jax.experimental.pallas import tpu as pltpu
 from jax.sharding import Mesh
 from jax.sharding import PartitionSpec as P
 
@@ -123,11 +126,221 @@
     )
 
 
+def exchange_kernel(
+    ring,
+    peers,
+    routed,
+    compact,
+    spread,
+    weights,
+    out,
+    held,
+    landed,
+    slots,
+    hidden,
+    sending,
+    arriving,
+    leaving,
+    held_sem,
+    out_send,
+    out_recv,
+    gather_send,
+    gather_recv,
+    ring_send,
+    ring_recv,
+    back_send,
+    back_recv,
+):
+    mesh_id = pl.DeviceIdType.MESH
+    at = lax.axis_index("seq_1")
+    me = lax.axis_index("expert")
+    right = {"seq_1": lax.rem(at + 1, ring)}
+    left = {"seq_1": lax.rem(at + ring - 1, ring)}
+    padded = routed.shape[0] // peers
+    width = routed.shape[1]
+    rows = compact.shape[0]
+    share = sending.shape[3]
+    half = ring // 2
+
+    def peer(j):
+        return {"expert": lax.rem(me + j, peers)}
+
+    barrier = pltpu.get_barrier_semaphore()
+    for device in [left, right] + [peer(j) for j in range(1, peers)]:
+        pl.semaphore_signal(barrier, inc=1, device_id=device, device_id_type=mesh_id)
+    fetch = pltpu.make_async_copy(weights, held, held_sem)
+    fetch.start()
+    pl.semaphore_wait(barrier, peers + 1)
+
+    started = []
+
+    def remote(source, target, send, recv, device):
+        copy = pltpu.make_async_remote_copy(
+            src_ref=source,
+            dst_ref=target,
+            send_sem=send,
+            recv_sem=recv,
+            device_id=device,
+            device_id_type=mesh_id,
+        )
+        copy.start()
+        started.append(copy)
+        return copy
+
+    outward = [
+        remote(
+            routed.at[pl.ds(j * padded, padded)],
+            landed.at[pl.ds(j * padded, padded)],
+            out_send.at[j],
+            out_recv.at[j],
+            peer(j),
+        )
+        for j in range(1, peers)
+    ]
+    landed[pl.ds(0, padded)] = routed[pl.ds(0, padded)]
+    for copy in outward:
+        copy.wait_recv()
+    slots[0] = jnp.dot(
+        compact[...], landed[...], preferred_element_type=jnp.float32
+    ).astype(jnp.bfloat16)
+
+    def forward_right(hop):
+        if hop < half:
+            source, target = slots.at[hop - 1], slots.at[hop]
+        else:
+            part = pl.ds(0, rows // 2)
+            source, target = slots.at[hop - 1, part], slots.at[hop, part]
+        return remote(source, target, gather_send.at[0, hop], gather_recv.at[0, hop], right)
+
+    def forward_left(hop):
+        begin, end = (ring - hop + 1) % ring, ring - hop
+        if hop < half:
+            source, target = slots.at[begin], slots.at[end]
+        else:
+            part = pl.ds(rows // 2, rows // 2)
+            source, target = slots.at[begin, part], slots.at[end, part]
+        return remote(source, target, gather_send.at[1, hop], gather_recv.at[1, hop], left)
+
+    def fill_hidden(slot):
+        over = (((1,), (1,)), ((), ()))
+        block = slots[slot]
+        gate = lax.dot_general(
+            block, held[:, pl.ds(0, width)], over, preferred_element_type=jnp.float32
+        )
+        upper = lax.dot_general(
+            block, held[:, pl.ds(width, width)], over, preferred_element_type=jnp.float32
+        )
+        hidden[slot] = (gate / (1.0 + jnp.exp(-gate)) * upper).astype(jnp.bfloat16)
+
+    def term(slot, quarter):
+        return jnp.dot(
+            hidden[slot],
+            held[:, pl.ds(2 * width + quarter * share, share)],
+            preferred_element_type=jnp.float32,
+        )
+
+    to_right, to_left = forward_right(1), forward_left(1)
+    fetch.wait()
+    fill_hidden(0)
+    rings = []
+    for step in range(ring - 1):
+        hop = step + 1
+        if hop <= half:
+            to_right.wait_recv()
+            to_left.wait_recv()
+            if hop < half:
+                to_right, to_left = forward_right(hop + 1), forward_left(hop + 1)
+            fill_hidden(hop)
+            if hop < half:
+                fill_hidden(ring - hop)
+        current = []
+        for quarter in (0, 2, 1, 3):
+            total = term(hop if quarter < 2 else ring - hop, quarter)
+            if step > 0:
+                rings[quarter].wait_recv()
+                total = total + arriving[quarter, step - 1].astype(jnp.float32)
+            sending[quarter, step] = total.astype(jnp.bfloat16)
+            current.append(
+                remote(
+                    sending.at[quarter, step],
+                    arriving.at[quarter, step],
+                    ring_send.at[quarter, step],
+                    ring_recv.at[quarter, step],
+                    right if quarter < 2 else left,
+                )
+            )
+        rings = [current[0], current[2], current[1], current[3]]
+    for quarter in (0, 2, 1, 3):
+        total = term(0, quarter)
+        rings[quarter].wait_recv()
+        total = (total + arriving[quarter, ring - 2].astype(jnp.float32)).astype(jnp.bfloat16)
+        leaving[:, pl.ds(quarter * share, share)] = jnp.dot(
+            spread[...], total, preferred_element_type=jnp.float32
+        ).astype(jnp.bfloat16)
+    back = [
+        remote(
+            leaving.at[pl.ds(j * padded, padded)],
+            out.at[pl.ds(j * padded, padded)],
+            back_send.at[j],
+            back_recv.at[j],
+            {"expert": lax.rem(me + peers - j, peers)},
+        )
+        for j in range(1, peers)
+    ]
+    out[pl.ds(0, padded)] = leaving[pl.ds(0, padded)]
+    for copy in back:
+        copy.wait_recv()
+    for copy in started:
+        copy.wait_send()
+
+
+def exchange(routed, weights, ring, peers, capacity):
+    padded = routed.shape[0] // peers
+    width = routed.shape[1]
+    inner = weights.shape[0]
+    outer = weights.shape[1] - 2 * width
+    rows = peers * capacity
+    share = outer // 4
+    row = jnp.arange(rows)
+    place = row // capacity * padded + row % capacity
+    compact = (place[:, None] == jnp.arange(peers * padded)[None, :]).astype(jnp.bfloat16)
+    dma = pltpu.SemaphoreType.DMA
+    kept = jnp.bfloat16
+    return pl.pallas_call(
+        functools.partial(exchange_kernel, ring, peers),
+        out_shape=jax.ShapeDtypeStruct((peers * padded, outer), kept),
+        in_specs=[pl.BlockSpec(memory_space=pltpu.VMEM)] * 3
+        + [pl.BlockSpec(memory_space=pl.ANY)],
+        out_specs=pl.BlockSpec(memory_space=pltpu.VMEM),
+        scratch_shapes=[
+            pltpu.VMEM(weights.shape, kept),
+            pltpu.VMEM(routed.shape, kept),
+            pltpu.VMEM((ring, rows, width), kept),
+            pltpu.VMEM((ring, rows, inner), kept),
+            pltpu.VMEM((4, ring - 1, rows, share), kept),
+            pltpu.VMEM((4, ring - 1, rows, share), kept),
+            pltpu.VMEM((peers * padded, outer), kept),
+            dma,
+            dma((peers,)),
+            dma((peers,)),
+            dma((2, ring // 2 + 1)),
+            dma((2, ring // 2 + 1)),
+            dma((4, ring - 1)),
+            dma((4, ring - 1)),
+            dma((peers,)),
+            dma((peers,)),
+        ],
+        compiler_params=pltpu.CompilerParams(
+            collective_id=0, has_side_effects=True, vmem_limit_bytes=40 << 20
+        ),
+    )(routed, compact, compact.T, weights)
+
+
 def mixture(patch_input, patch_state, expert_ids, moe_gain, w_router, weights):
-    width = patch_input.shape[1]
     patch_cap = patch_state.shape[0]
     experts = w_router.shape[1]
     capacity = 12 * patch_cap // (5 * experts)
+    padded = -(-capacity // 16) * 16
     widened = patch_state.astype(jnp.float32)
     scale = lax.rsqrt(jnp.mean(widened * widened, axis=-1, keepdims=True) + epsilon)
     normed = (widened * scale * moe_gain).astype(jnp.bfloat16)
@@ -135,31 +348,14 @@
     picked = expert_ids[:, :, None] == jnp.arange(experts, dtype=jnp.int32)[None, None, :]
     gates = softmax_rows(jnp.sum(jnp.where(picked, logits[:, None, :], 0.0), axis=2))
     slot_number = route_slots(expert_ids, experts)
-    target = expert_ids * capacity + slot_number
-    places = jnp.arange(experts * capacity, dtype=jnp.int32)
+    relative = lax.rem(expert_ids + experts - lax.axis_index("expert"), experts)
+    target = relative * padded + slot_number
+    places = jnp.arange(experts * padded, dtype=jnp.int32)
     chosen = target[None, :, :] == places[:, None, None]
     dispatch = jnp.sum(chosen.astype(jnp.bfloat16), axis=2)
     sent = (patch_input.astype(jnp.float32) * scale).astype(jnp.bfloat16)
     routed = jnp.dot(dispatch, sent, preferred_element_type=jnp.float32).astype(jnp.bfloat16)
-    arrived = lax.all_to_all(
-        routed.reshape(experts, capacity, width), "expert", split_axis=0, concat_axis=0, tiled=True
-    )
-    rows = lax.all_gather(
-        arrived.reshape(experts * capacity, width), "seq_1", axis=0, tiled=True
-    )
-    over = (((1,), (1,)), ((), ()))
-    gate = lax.dot_general(rows, weights[:, :width], over, preferred_element_type=jnp.float32)
-    upper = lax.dot_general(
-        rows, weights[:, width : 2 * width], over, preferred_element_type=jnp.float32
-    )
-    hidden = (jax.nn.silu(gate) * upper).astype(jnp.bfloat16)
-    term = jnp.dot(hidden, weights[:, 2 * width :], preferred_element_type=jnp.float32).astype(
-        jnp.bfloat16
-    )
-    summed = lax.psum_scatter(term, "seq_1", scatter_dimension=0, tiled=True)
-    returned = lax.all_to_all(
-        summed.reshape(experts, capacity, -1), "expert", split_axis=0, concat_axis=0, tiled=True
-    ).reshape(experts * capacity, -1)
+    returned = exchange(routed, weights, lax.axis_size("seq_1"), experts, capacity)
     weighted = jnp.sum(jnp.where(chosen, gates[None], 0.0), axis=2)
     high = weighted.astype(jnp.bfloat16)
     low = (weighted - high.astype(jnp.float32)).astype(jnp.bfloat16)

time: 174 us -> 153 us (0.88)
  Pallas kernels: 0 us -> 60.1 us
  blocking collectives: 33.9 us -> 0 us
  waiting for transfers between devices: 53.2 us -> 26.7 us
  matrix products: 37.9 us -> 26.2 us
  starting transfers between devices: 16.8 us -> 8.78 us
  local copies, waits for them, and re-layouts: 8.06 us -> 5.98 us
    pallas_call x0 -> x1, Pallas kernels: none -> 60.1 us  [exchange(): pl.pallas_call(functools.partial(exchange_kernel, ring, peers), out_shape...]
    reduce_scatter x1 -> x0, waiting for transfers between devices: 44.1 us -> none  [mixture(): summed = lax.psum_scatter(term, 'seq_1', scatter_dimension=0, tiled=True)]
    all_gather x1, waiting for transfers between devices: 0.01 us -> 26.7 us  [per_device(): lax.all_gather(folded_weights(w_up, moe_gain, w_in, w_down), 'seq_0', axi...]
    all_gather x1 -> x0, blocking collectives: 25 us -> none  [mixture(): lax.all_gather(arrived.reshape(experts * capacity, width), 'seq_1', axis=...]
    dot_general x2 -> x0, matrix products: 11.2 us -> none  [the longest x1 7.78 us: mixture(): jnp.dot(hidden, weights[:, 2 * width:], preferred_element_type=jnp.float32)]
    all_to_all x1 -> x0, waiting for transfers between devices: 9.08 us -> none  [mixture(): lax.all_to_all(summed.reshape(experts, capacity, -1), 'expert', split_axi...]
    all_to_all x1 -> x0, blocking collectives: 8.88 us -> none  [mixture(): lax.all_to_all(routed.reshape(experts, capacity, width), 'expert', split_...]
    all_to_all x1 -> x0, starting transfers between devices: 7.96 us -> none  [mixture(): lax.all_to_all(summed.reshape(experts, capacity, -1), 'expert', split_axi...]
  transfers between devices with their start and end apart: 5 -> 3, of which waited for: 2 -> 1; matrix products, arithmetic and copies ran while one was open for 19% -> 22% of each run, Pallas kernels for 0% -> 0%
where the time goes in v2:
time: 153 us; the launch traced here: 152 us
  Pallas kernels  60.1 us (39%)
  waiting for transfers between devices  26.7 us (17%)
  matrix products  26.2 us (17%)
  between operations  14.6 us (10%)
  other arithmetic  9.9 us (6%)
  starting transfers between devices  8.78 us (6%)
  local copies, waits for them, and re-layouts  5.98 us (4%)
    pallas_call x1, Pallas kernels, exchange(): pl.pallas_call(functools.partial(exchange_kernel, ring, peers), out_shape...  60.1 us
    all_gather x1, waiting for transfers between devices, per_device(): lax.all_gather(folded_weights(w_up, moe_gain, w_in, w_down), 'seq_0', axi...  26.7 us
    ppermute x2, starting transfers between devices, passed_along(): return lax.ppermute(x, axis, pairs)  8.75 us
    sub x1, matrix products, softmax_rows(): raised = jnp.exp(scores - highest)  6.01 us
    dot_general x3, matrix products, attend(): jnp.einsum('hqk,hkd->hqd', weights, values, preferred_element_type=jnp.fl...  4.95 us
    dot_general x2, matrix products, per_device(): jnp.dot(moved, w_qkv[:, model_width:], preferred_element_type=jnp.float32)  3.51 us
  transfers between devices with their start and end apart: 3, of which 1 were waited for; matrix products, arithmetic and copies ran while one was open for 22% of the time, Pallas kernels for 0%

profile of v2, /device:TPU:1, one launch (start us, length us, event | category | flops | bytes accessed | tf_op | source)
XLA Modules:
  0.0 152.3 jit_solution(15549598143974370865)
XLA Ops:
  7.2 1.2 fusion.34
  8.4 1.8 %fusion.36 = bf16[256,512]{1,0:T(8,128)(2,1)} fusion(bf16[256,512]{1,0:T(8,128)(2,1)} %param.17, f32[512]{0:T(512)} %param.20, f32[256]{0:T(256)S(1)} %add_rsqrt_fusion.1), kind=kLoop, calls=%fused_computation.63 | loop fusion | flops 524288 | bytes 527360 | tf_op jit(solution)/shard_map/convert_element_type | solution.py:393
  10.2 4.8 %collective-permute-start.1 = (bf16[256,512]{1,0:T(8,128)(2,1)}, bf16[256,512]{1,0:T(8,128)(2,1)}, u32[]{:S(2)}, u32[]{:S(2)}) collective-permute-start(bf16[256,512]{1,0:T(8,128)(2,1)} %fusion.36), channel_id=1, source_target_pairs={{0,1},{1,2},{2,3},{3,4},{4,5},{5,6},{6,7},{7,8},{8,9},{9,10},{10,1... | collective-permute-start | bytes 786440 | tf_op jit(solution)/shard_map/ppermute | solution.py:26
  15.0 3.9 %collective-permute-start = (bf16[256,512]{1,0:T(8,128)(2,1)}, bf16[256,512]{1,0:T(8,128)(2,1)}, u32[]{:S(2)}, u32[]{:S(2)}) collective-permute-start(bf16[256,512]{1,0:T(8,128)(2,1)} %fusion.36), channel_id=1, source_target_pairs={{0,2},{1,3},{2,4},{3,5},{4,6},{5,7},{6,8},{7,9},{8,10},{9,11},{10,... | collective-permute-start | bytes 786440 | tf_op jit(solution)/shard_map/ppermute | solution.py:26
  18.9 2.6 %fusion.24 = bf16[192,512]{1,0:T(8,128)(2,1)S(1)} fusion(bf16[512,2048]{1,0:T(8,128)(2,1)} %param.25, f32[2048]{0:T(1024)} %param.26, bf16[1,2048,2,192]{1,3,2,0:T(8,128)(2,1)} %param.28), kind=kOutput, calls=%fused_computation.43 | convolution fusion | flops 405897216 | bytes 3088384 | tf_op jit(solution)/shard_map/dot_general | solution.py:123
  21.6 0.9 fusion.25
  22.7 1.1 pad_maximum_fusion.1
  23.9 0.3 reduce-window.9
  24.6 0.6 reduce_sum.114
  25.3 1.5 convolution_convert_fusion
  27.8 0.7 iota_compare_fusion.7
  28.6 0.8 copy.77
  29.4 0.9 compare_and_fusion
  30.3 1.8 %convolution_convert_fusion.3 = bf16[256,1024]{1,0:T(8,128)(2,1)S(1)} fusion(bf16[256,512]{1,0:T(8,128)(2,1)} %collective-permute-done.1, bf16[512,1536]{1,0:T(8,128)(2,1)} %param.21), kind=kOutput, calls=%fused_computation.23 | convolution fusion | flops 268697600 | bytes 1835008 | tf_op jit(solution)/shard_map/dot_general | solution.py:402
  32.1 1.8 %convolution_convert_fusion.4 = bf16[256,1024]{1,0:T(8,128)(2,1)S(1)} fusion(bf16[256,512]{1,0:T(8,128)(2,1)} %collective-permute-done, bf16[512,1536]{1,0:T(8,128)(2,1)} %param.21), kind=kOutput, calls=%fused_computation.24 | convolution fusion | flops 268697600 | bytes 1835008 | tf_op jit(solution)/shard_map/dot_general | solution.py:402
  34.1 0.3 copy.79
  34.4 0.3 copy.78
  34.7 6.0 %fusion.78 = (f32[8,256]{1,0:T(8,128)S(1)}, f32[8,256,768]{2,1,0:T(8,128)}) fusion(pred[256,768]{1,0:T(8,128)(4,1)} %compare_and_fusion, bf16[8,256,64]{1,2,0:T(8,128)(2,1)} %bitcast.87, bf16[8,768,64]{1,2,0:T(8,128)(2,1)S(1)} %bitcast.84), kind=kOutput, calls=%fused_computation.140 | convolution fusion | flops 207618816 | bytes 7544832 | tf_op jit(solution)/shard_map/sub | solution.py:40
  40.7 4.1 %fusion.17 = bf16[8,256,64]{1,2,0:T(8,128)(2,1)S(1)} fusion(bf16[8,768,64]{1,2,0:T(8,128)(2,1)S(1)} %bitcast.83, f32[8,256,768]{2,1,0:T(8,128)} %get-tuple-element.9, f32[8,256]{1,0:T(8,128)S(1)} %get-tuple-element.8), kind=kOutput, calls=%fused_computation.33 | convolution fusion | flops 204603392 | bytes 7348224 | tf_op jit(solution)/shard_map/hqk,hkd->hqd/dot_general | solution.py:58
  44.8 0.4 fusion.37
  45.2 0.3 convolution_convert_fusion.6
  45.7 0.4 convolution_convert_fusion.2
  46.5 1.8 %select_reduce_fusion = bf16[40,512]{1,0:T(8,128)(2,1)S(1)} fusion(pred[40,256]{1,0:T(8,128)(4,1)S(1)} %iota_compare_fusion.4, bf16[256,512]{1,0:T(8,128)(2,1)S(1)} %get-tuple-element.11), kind=kLoop, calls=%fused_computation.3 | loop fusion | flops 10465280 | bytes 313344 | tf_op jit(solution)/shard_map/reduce_max | solution.py:74
  49.2 0.6 convolution_bitcast_fusion
  50.0 2.2 %multiply_reduce_fusion = (f32[40]{0:T(128)S(1)}, f32[40,2048]{1,0:T(8,128)S(1)}) fusion(bf16[40,512]{1,0:T(8,128)(2,1)S(1)} %select_convert_fusion, bf16[512,2048]{1,0:T(8,128)(2,1)} %param.25), kind=kOutput, calls=%fused_computation.69 | convolution fusion | flops 84213720 | bytes 2465952 | tf_op jit(solution)/shard_map/dot_general | solution.py:90
  52.2 0.3 fusion.43
  52.9 26.7 %all-gather.2.cloned.1.call-done.weights = bf16[768,3072]{1,0:T(8,128)(2,1)} async-done(((bf16[192,3072]{1,0:T(8,128)(2,1)}), bf16[768,3072]{1,0:T(8,128)(2,1)}) %all-gather.2.cloned.1.call-update) | async-done | bytes 4718608 | tf_op jit(solution)/shard_map/all_gather | solution.py:388
  79.7 2.3 %copy-done.1 = bf16[768,3072]{1,0:T(8,128)(2,1)S(1)} copy-done((bf16[768,3072]{1,0:T(8,128)(2,1)S(1)}, bf16[768,3072]{1,0:T(8,128)(2,1)}, u32[]{:S(2)}) %copy-start.1) | copy-done | bytes 4718616
  82.0 60.1 %shard_map.176 = bf16[128,2048]{1,0:T(8,128)(2,1)S(1)} custom-call(bf16[128,512]{1,0:T(8,128)(2,1)S(1)} %convolution_convert_fusion.7.routed, bf16[96,128]{1,0:T(8,128)(2,1)S(1)} %fusion.55.compact, bf16[128,96]{1,0:T(8,128)(2,1)S(1)} %fusion.54.spread, bf16[768,3072]{1,0:T(8,128)(2,1)S(1)} %copy-done.1), custom_call_target="tpu_custom_call" | custom-call | tf_op jit(solution)/shard_map/pallas_call | solution.py:309
  142.5 0.8 convolution_convert_fusion.8
  143.9 0.3 convolution_convert_fusion.5
  144.4 1.0 fusion.16
  (91 shorter events, 5.0 us)
Async XLA Ops:
  7.2 38.6 %copy-start = (bf16[512,1024]{1,0:T(8,128)(2,1)S(1)}, bf16[512,1024]{1,0:T(8,128)(2,1)}, u32[]{:S(2)}) copy-start(bf16[512,1024]{1,0:T(8,128)(2,1)} %param.24) | copy-start | bytes 3145732
  7.2 72.5 %all-gather.2.cloned.1.call-start = ((), (), s32[]{:S(2)}) async-start(), calls=%async_computation | async-start | bytes 5898240 | tf_op jit(solution)/shard_map/all_gather | solution.py:388
  10.2 11.4 %copy-start.3 = (bf16[512,2048]{1,0:T(8,128)(2,1)S(1)}, bf16[512,2048]{1,0:T(8,128)(2,1)}, u32[]{:S(2)}) copy-start(bf16[512,2048]{1,0:T(8,128)(2,1)} %param.25) | copy-start | bytes 6291460
  10.2 11.4 %copy-start.12 = (f32[2048]{0:T(1024)S(1)}, f32[2048]{0:T(1024)}, u32[]{:S(2)}) copy-start(f32[2048]{0:T(1024)} %param.26) | copy-start | bytes 24580
  10.2 11.4 %copy-start.14 = (bf16[1,2048,2,192]{1,3,2,0:T(8,128)(2,1)S(1)}, bf16[1,2048,2,192]{1,3,2,0:T(8,128)(2,1)}, u32[]{:S(2)}) copy-start(bf16[1,2048,2,192]{1,3,2,0:T(8,128)(2,1)} %param.28) | copy-start | bytes 4718596
  10.2 20.1 %collective-permute-start.1 = (bf16[256,512]{1,0:T(8,128)(2,1)}, bf16[256,512]{1,0:T(8,128)(2,1)}, u32[]{:S(2)}, u32[]{:S(2)}) collective-permute-start(bf16[256,512]{1,0:T(8,128)(2,1)} %fusion.36), channel_id=1, source_target_pairs={{0,1},{1,2},{2,3},{3,4},{4,5},{5,6},{6,7},{7,8},{8,9},{9,10},{10,1... | collective-permute-start | bytes 786440 | tf_op jit(solution)/shard_map/ppermute | solution.py:26
  15.0 17.1 %collective-permute-start = (bf16[256,512]{1,0:T(8,128)(2,1)}, bf16[256,512]{1,0:T(8,128)(2,1)}, u32[]{:S(2)}, u32[]{:S(2)}) collective-permute-start(bf16[256,512]{1,0:T(8,128)(2,1)} %fusion.36), channel_id=1, source_target_pairs={{0,2},{1,3},{2,4},{3,5},{4,6},{5,7},{6,8},{7,9},{8,10},{9,11},{10,... | collective-permute-start | bytes 786440 | tf_op jit(solution)/shard_map/ppermute | solution.py:26
  21.6 1.1 copy-start.6
  22.5 1.4 copy-start.13
  22.5 2.8 %copy-start.4 = (bf16[512,1536]{1,0:T(8,128)(2,1)S(1)}, bf16[512,1536]{1,0:T(8,128)(2,1)}, u32[]{:S(2)}) copy-start(bf16[512,1536]{1,0:T(8,128)(2,1)} %param.21) | copy-start | bytes 4718596
  23.9 3.0 %copy-start.11 = (s32[40,2]{0,1:T(2,128)S(1)}, s32[40,2]{0,1:T(2,128)}, u32[]{:S(2)}) copy-start(s32[40,2]{0,1:T(2,128)} %param.19) | copy-start | bytes 964
  40.7 4.1 %copy-start.5 = (bf16[256,512]{1,0:T(8,128)(2,1)S(1)}, bf16[256,512]{1,0:T(8,128)(2,1)}, u32[]{:S(2)}) copy-start(bf16[256,512]{1,0:T(8,128)(2,1)} %param.17) | copy-start | bytes 786436
  40.7 4.1 %copy-start.15 = (bf16[512,512]{1,0:T(8,128)(2,1)S(1)}, bf16[512,512]{1,0:T(8,128)(2,1)}, u32[]{:S(2)}) copy-start(bf16[512,512]{1,0:T(8,128)(2,1)} %param.22) | copy-start | bytes 1572868
  40.7 4.5 %copy-start.16 = (bf16[512,512]{1,0:T(8,128)(2,1)S(1)}, bf16[512,512]{1,0:T(8,128)(2,1)}, u32[]{:S(2)}) copy-start(bf16[512,512]{1,0:T(8,128)(2,1)} %param.31) | copy-start | bytes 1572868
  40.7 4.5 %copy-start.17 = (f32[512]{0:T(512)S(1)}, f32[512]{0:T(512)}, u32[]{:S(2)}) copy-start(f32[512]{0:T(512)} %param.30) | copy-start | bytes 6148
  45.6 2.8 %copy-start.8 = (bf16[512,512]{1,0:T(8,128)(2,1)S(1)}, bf16[512,512]{1,0:T(8,128)(2,1)}, u32[]{:S(2)}) copy-start(bf16[512,512]{1,0:T(8,128)(2,1)} %param.23) | copy-start | bytes 1572868
  49.1 3.1 %copy-start.10 = (f32[2048,8]{0,1:T(8,128)S(1)}, f32[2048,8]{0,1:T(8,128)}, u32[]{:S(2)}) copy-start(f32[2048,8]{0,1:T(8,128)} %param.27) | copy-start | bytes 196612
  79.7 2.3 %copy-start.1 = (bf16[768,3072]{1,0:T(8,128)(2,1)S(1)}, bf16[768,3072]{1,0:T(8,128)(2,1)}, u32[]{:S(2)}) copy-start(bf16[768,3072]{1,0:T(8,128)(2,1)} %all-gather.2.cloned.1.call-done.weights) | copy-start | bytes 14155780
  82.0 60.5 %copy-start.2 = (bf16[2048,1024]{1,0:T(8,128)(2,1)S(1)}, bf16[2048,1024]{1,0:T(8,128)(2,1)}, u32[]{:S(2)}) copy-start(bf16[2048,1024]{1,0:T(8,128)(2,1)} %param.32) | copy-start | bytes 12582916
  142.5 1.0 copy-start.7
  143.4 1.0 copy-start.9
Sparse Core Ops, SparseCore 0:
  24.0 55.5 all-gather.1

commit v3 on v0

v3 whole, which is shorter than its diff:
```python
import functools

import jax
import jax.numpy as jnp
from jax import lax
from jax.experimental import pallas as pl
from jax.experimental.pallas import tpu as pltpu
from jax.sharding import Mesh
from jax.sharding import PartitionSpec as P

HEADS = 8
HEAD = 64
PAIR = 2 * HEAD
PADDED = 16
LAG = 3
SEQ = ("seq_0", "seq_1")
SEQ_EXPERT = ("seq_0", "seq_1", "expert")

epsilon = 1e-06
very_negative = -1e30
bf16 = jnp.bfloat16
f32 = jnp.float32


def iota(shape, dimension):
    return lax.broadcasted_iota(jnp.int32, shape, dimension)


def mul(a, b):
    return jnp.dot(a, b, preferred_element_type=f32)


def mul_over_last(a, b):
    return lax.dot_general(a, b, (((1,), (1,)), ((), ())), preferred_element_type=f32)


def rms_scale(inputs, gain_vector):
    widened = inputs.astype(f32)
    return (
        widened
        * lax.rsqrt(jnp.mean(widened * widened, axis=-1, keepdims=True) + epsilon)
        * gain_vector
    )


def in_head(shape, h):
    lane = iota(shape, len(shape) - 1)
    return (lane >= h * HEAD) & (lane < (h + 1) * HEAD)


def step_kernel(
    sizes,
    states,
    flags,
    ids,
    enc_gain,
    moe_gain,
    dec_gain,
    w_router,
    folded,
    w_down,
    w_qkv_hbm,
    w_out_hbm,
    w_xq_hbm,
    w_xkv_hbm,
    w_up_hbm,
    w_dq_hbm,
    w_dkv_hbm,
    w_do_hbm,
    bytes_out,
    patch_out,
    w_qkv,
    w_out,
    w_xq,
    w_xkv,
    w_up,
    w_dq,
    w_dkv,
    w_do,
    up_held,
    down_held,
    halo,
    keys,
    values,
    mixing,
    routed,
    landed,
    slots,
    hidden,
    sending,
    arriving,
    leaving,
    returned,
    fetch_sem,
    halo_send,
    halo_recv,
    weight_send,
    weight_recv,
    out_send,
    out_recv,
    gather_send,
    gather_recv,
    ring_send,
    ring_recv,
    back_send,
    back_recv,
):
    groups, ring, peers = sizes
    mesh_id = pl.DeviceIdType.MESH
    plane = lax.axis_index("seq_0")
    at = lax.axis_index("seq_1")
    me = lax.axis_index("expert")
    right = {"seq_1": lax.rem(at + 1, ring)}
    left = {"seq_1": lax.rem(at + ring - 1, ring)}
    up = {"seq_0": lax.rem(plane + 1, groups)}
    down = {"seq_0": lax.rem(plane + groups - 1, groups)}
    count, width = states.shape
    slot_count, outer = patch_out.shape
    share = folded.shape[1]
    capacity = slots.shape[1] // peers
    rows = peers * capacity
    quarter_width = outer // 4
    half = ring // 2

    def peer(j):
        return {"expert": lax.rem(me + j, peers)}

    def stretch(by):
        moved = me + by + peers
        row = at + moved // peers - 1 + ring
        return {
            "seq_0": lax.rem(plane + row // ring - 1 + groups, groups),
            "seq_1": lax.rem(row, ring),
            "expert": lax.rem(moved, peers),
        }

    partners = [up, down, right, left] + [peer(j) for j in range(1, peers)]
    partners += [stretch(1), stretch(2), stretch(-1), stretch(-2)]
    barrier = pltpu.get_barrier_semaphore()
    for device in partners:
        pl.semaphore_signal(barrier, inc=1, device_id=device, device_id_type=mesh_id)

    fetches = {}
    for number, (name, source, target) in enumerate(
        [
            ("qkv", w_qkv_hbm, w_qkv),
            ("out", w_out_hbm, w_out),
            ("xkv", w_xkv_hbm, w_xkv),
            ("xq", w_xq_hbm, w_xq),
            ("w_up", w_up_hbm, w_up),
            ("up", folded, up_held.at[:, pl.ds(0, share)]),
            ("down", w_down, down_held.at[pl.ds(0, share)]),
            ("dq", w_dq_hbm, w_dq),
            ("dkv", w_dkv_hbm, w_dkv),
            ("do", w_do_hbm, w_do),
        ]
    ):
        fetches[name] = pltpu.make_async_copy(source, target, fetch_sem.at[number])
        fetches[name].start()
    pl.semaphore_wait(barrier, len(partners))

    started = []

    def remote(source, target, send, recv, device):
        copy = pltpu.make_async_remote_copy(
            src_ref=source,
            dst_ref=target,
            send_sem=send,
            recv_sem=recv,
            device_id=device,
            device_id_type=mesh_id,
        )
        copy.start()
        started.append(copy)
        return copy

    near = remote(states, halo.at[1], halo_send.at[0], halo_recv.at[0], stretch(1))
    far = remote(states, halo.at[0], halo_send.at[1], halo_recv.at[1], stretch(2))

    def weight_copy(stage, direction, source, target):
        return remote(
            source,
            target,
            weight_send.at[direction, stage],
            weight_recv.at[direction, stage],
            up if direction == 0 else down,
        )

    def up_slice(slot):
        return up_held.at[:, pl.ds(slot * share, share)]

    def down_slice(slot, part, rows_from=0, rows_count=None):
        return down_held.at[
            pl.ds(slot * share + rows_from, rows_count or share),
            pl.ds(part * (outer // 2), outer // 2),
        ]

    def pass_up_first():
        return [weight_copy(0, d, folded, up_slice((1, 3)[d])) for d in range(2)]

    def pass_up_second():
        copies = []
        for d in range(2):
            begin = up_held.at[d, pl.ds((1, 3)[d] * share, share)]
            copies.append(weight_copy(1, d, begin, up_held.at[d, pl.ds(2 * share, share)]))
        return copies

    def pass_down_first(part):
        source = w_down.at[:, pl.ds(part * (outer // 2), outer // 2)]
        return [
            weight_copy(2 + 2 * part, d, source, down_slice((1, 3)[d], part)) for d in range(2)
        ]

    def pass_down_second(part):
        return [
            weight_copy(
                3 + 2 * part,
                d,
                down_slice((1, 3)[d], part, d * (share // 2), share // 2),
                down_slice(2, part, d * (share // 2), share // 2),
            )
            for d in range(2)
        ]

    def landed_all(copies):
        for copy in copies:
            copy.wait_recv()

    up_first = pass_up_first()
    down_first = pass_down_first(0)

    def keep_pairs(number, projected):
        kept = projected.astype(bf16)
        keys[number] = kept[:, :width]
        values[number] = kept[:, width:]

    fetches["qkv"].wait()
    normed = rms_scale(states[...], enc_gain[...]).astype(bf16)
    queries = (mul(normed, w_qkv[:, pl.ds(0, width)]).astype(bf16).astype(f32) * 0.125).astype(bf16)
    keep_pairs(2, mul(normed, w_qkv[:, pl.ds(width, 2 * width)]))
    near.wait_recv()
    earlier = rms_scale(halo[1], enc_gain[...]).astype(bf16)
    keep_pairs(1, mul(earlier, w_qkv[:, pl.ds(width, 2 * width)]))
    far.wait_recv()
    earlier = rms_scale(halo[0], enc_gain[...]).astype(bf16)
    keep_pairs(0, mul(earlier, w_qkv[:, pl.ds(width, 2 * width)]))

    place = (plane * ring + at) * peers + me
    no_near = jnp.where(place < 1, very_negative, 0.0).astype(f32)
    no_far = jnp.where(place < 2, very_negative, 0.0).astype(f32)
    causal = iota((count, count), 1) <= iota((count, count), 0)
    first_half = iota((count, PAIR), 1) < HEAD
    for pair in range(HEADS // 2):
        columns = slice(pair * PAIR, (pair + 1) * PAIR)
        outs = []
        for side in range(2):
            asked = jnp.where(first_half == (side == 0), queries[:, columns].astype(f32), 0.0)
            asked = asked.astype(bf16)
            own = mul_over_last(asked, keys[2, :, columns])
            back_two = mul_over_last(asked, keys[0, :, columns]) + no_far
            back_one = mul_over_last(asked, keys[1, :, columns]) + no_near
            shared = jnp.where(causal, own, back_two)
            highest = jnp.maximum(
                jnp.max(shared, axis=-1, keepdims=True), jnp.max(back_one, axis=-1, keepdims=True)
            )
            shared = jnp.exp(shared - highest)
            back_one = jnp.exp(back_one - highest)
            total = jnp.sum(shared, axis=-1, keepdims=True) + jnp.sum(
                back_one, axis=-1, keepdims=True
            )
            mixed = (
                mul(jnp.where(causal, shared, 0.0).astype(bf16), values[2, :, columns])
                + mul(jnp.where(causal, 0.0, shared).astype(bf16), values[0, :, columns])
                + mul(back_one.astype(bf16), values[1, :, columns])
            )
            outs.append(mixed / total)
        mixing[:, columns] = jnp.where(first_half, outs[0], outs[1]).astype(bf16)
        if pair == 1:
            landed_all(up_first)
            up_second = pass_up_second()
    fetches["out"].wait()
    encoded = (states[...].astype(f32) + mul(mixing[...], w_out[...])).astype(bf16)

    opened = flags[...].astype(f32)
    row_at = iota((count, count), 0)
    column_at = iota((count, count), 1)
    opened_wide = jnp.broadcast_to(opened, (8, count)).astype(bf16)
    number_row = mul(opened_wide, (row_at <= column_at).astype(f32).astype(bf16))[:1] - 1.0
    next_row = mul(opened_wide, (row_at <= column_at + 1).astype(f32).astype(bf16))[:1] - 1.0
    last_row = (next_row > number_row) | (iota((1, count), 1) == count - 1)
    seen = (column_at <= row_at) & (opened > 0.5)
    number_column = jnp.sum(seen.astype(f32), axis=1, keepdims=True) - 1.0
    begin = jnp.max(jnp.where(seen, column_at, -1).astype(f32), axis=1, keepdims=True)
    depth = iota((count, 1), 0).astype(f32) - begin
    scanned = encoded.astype(f32)
    reach = 1
    while reach < count:
        moved = pltpu.roll(scanned, reach, 0)
        scanned = jnp.where(depth >= reach, jnp.maximum(scanned, moved), scanned)
        reach *= 2
    member = iota((slot_count, count), 0).astype(f32) == number_row
    live = jnp.max(member.astype(f32), axis=1, keepdims=True)
    chosen_last = jnp.where(member & last_row, 1.0, 0.0).astype(bf16)
    pooled = mul(chosen_last, scanned.astype(bf16))
    fetches["xkv"].wait()
    pairs = mul(encoded, w_xkv[...]).astype(bf16)
    fetches["xq"].wait()
    asked = mul(pooled.astype(bf16), w_xq[...]).astype(bf16).astype(f32) * 0.125
    stacked = jnp.concatenate(
        [jnp.where(in_head(asked.shape, h), asked, 0.0) for h in range(HEADS)], axis=0
    ).astype(bf16)
    bias = jnp.where(member, 0.0, very_negative)
    scores = mul_over_last(stacked, pairs[:, :width]) + jnp.concatenate([bias] * HEADS, axis=0)
    raised = jnp.exp(scores - jnp.max(scores, axis=-1, keepdims=True))
    weighed = (raised / jnp.sum(raised, axis=-1, keepdims=True)).astype(bf16)
    spread_out = mul(weighed, pairs[:, width:])
    patch_mix = pooled
    for h in range(HEADS):
        part = spread_out[h * slot_count : (h + 1) * slot_count]
        patch_mix = patch_mix + jnp.where(in_head(part.shape, h), part, 0.0)
    patch_input = jnp.where(live > 0.5, patch_mix, 0.0).astype(bf16)
    fetches["w_up"].wait()
    state = mul(patch_input, w_up[...]).astype(bf16).astype(f32)
    scale = lax.rsqrt(jnp.mean(state * state, axis=-1, keepdims=True) + epsilon)

    lane = iota((slot_count, peers * PADDED), 1)
    expert = [ids[:, k : k + 1] for k in range(2)]
    named = [jnp.where(lane == expert[k], 1.0, 0.0) for k in range(2)]
    before = jnp.where(iota((slot_count,) * 2, 1) < iota((slot_count,) * 2, 0), 1.0, 0.0)
    counted = mul(before.astype(bf16), (named[0] + named[1]).astype(bf16))
    target = []
    for k in range(2):
        rank = jnp.sum(counted * named[k], axis=1, keepdims=True).astype(jnp.int32)
        relative = expert[k] - me
        relative = jnp.where(relative < 0, relative + peers, relative)
        target.append(relative * PADDED + rank)
    placed = jnp.where((lane == target[0]) | (lane == target[1]), 1.0, 0.0)
    sent = (patch_input.astype(f32) * scale).astype(bf16)
    routed[...] = mul(jnp.transpose(placed).astype(bf16), sent).astype(bf16)

    outward = [
        remote(
            routed.at[pl.ds(j * PADDED, PADDED)],
            landed.at[pl.ds(j * PADDED, PADDED)],
            out_send.at[j],
            out_recv.at[j],
            peer(j),
        )
        for j in range(1, peers)
    ]
    landed[pl.ds(0, PADDED)] = routed[pl.ds(0, PADDED)]
    landed_all(down_first)
    down_second = pass_down_second(0)
    last_first = pass_down_first(1)

    patch_normed = (state * scale * moe_gain[...]).astype(bf16)
    logits = jnp.dot(
        patch_normed.astype(f32),
        w_router[...],
        precision=lax.Precision.HIGHEST,
        preferred_element_type=f32,
    )
    column = iota(logits.shape, 1)
    picked = [
        jnp.sum(jnp.where(column == expert[k], logits, 0.0), axis=1, keepdims=True)
        for k in range(2)
    ]
    top = jnp.maximum(picked[0], picked[1])
    raised = [jnp.exp(value - top) for value in picked]
    gates = [value / (raised[0] + raised[1]) for value in raised]
    weighted = jnp.where(lane == target[0], gates[0], 0.0) + jnp.where(
        lane == target[1], gates[1], 0.0
    )
    weighted_high = weighted.astype(bf16)
    weighted_low = (weighted - weighted_high.astype(f32)).astype(bf16)
    fetches["dq"].wait()
    byte_normed = rms_scale(encoded, dec_gain[...]).astype(bf16)
    byte_queries = (mul(byte_normed, w_dq[...]).astype(bf16).astype(f32) * 0.125).astype(bf16)

    def place_of(index):
        return (index >> 4) * capacity + (index & (PADDED - 1))

    def used(index):
        return (index & (PADDED - 1)) < capacity

    wide = iota((rows, peers * PADDED), 1)
    compact = jnp.where((iota(wide.shape, 0) == place_of(wide)) & used(wide), 1.0, 0.0)
    tall = iota((peers * PADDED, rows), 0)
    spread = jnp.where((iota(tall.shape, 1) == place_of(tall)) & used(tall), 1.0, 0.0)
    spread = spread.astype(bf16)

    landed_all(outward)
    slots[0] = mul(compact.astype(bf16), landed[...]).astype(bf16)

    def forward_right(hop):
        if hop < half:
            source, end = slots.at[hop - 1], slots.at[hop]
        else:
            part = pl.ds(0, rows // 2)
            source, end = slots.at[hop - 1, part], slots.at[hop, part]
        return remote(source, end, gather_send.at[0, hop], gather_recv.at[0, hop], right)

    def forward_left(hop):
        begin, finish = (ring - hop + 1) % ring, ring - hop
        if hop < half:
            source, end = slots.at[begin], slots.at[finish]
        else:
            part = pl.ds(rows // 2, rows // 2)
            source, end = slots.at[begin, part], slots.at[finish, part]
        return remote(source, end, gather_send.at[1, hop], gather_recv.at[1, hop], left)

    def fill_hidden(slot):
        block = slots[slot]
        gate = mul_over_last(block, up_held[0])
        upper = mul_over_last(block, up_held[1])
        hidden[slot] = (gate / (1.0 + jnp.exp(-gate)) * upper).astype(bf16)

    def term(slot, quarter):
        return mul(hidden[slot], down_held[:, pl.ds(quarter * quarter_width, quarter_width)])

    pending = [None] * 4

    def advance(quarter, step):
        total = term(step + 1 if quarter % 2 == 0 else ring - 1 - step, quarter)
        if step > 0:
            pending[quarter].wait_recv()
            total = total + arriving[quarter, step - 1].astype(f32)
        sending[quarter, step] = total.astype(bf16)
        pending[quarter] = remote(
            sending.at[quarter, step],
            arriving.at[quarter, step],
            ring_send.at[quarter, step],
            ring_recv.at[quarter, step],
            right if quarter % 2 == 0 else left,
        )

    to_right, to_left = forward_right(1), forward_left(1)
    fetches["up"].wait()
    landed_all(up_second)
    fill_hidden(0)
    for tick in range(ring - 1 + LAG):
        hop = tick + 1
        if hop <= half:
            landed_all([to_right, to_left])
            if hop < half:
                to_right, to_left = forward_right(hop + 1), forward_left(hop + 1)
            fill_hidden(hop)
            if hop < half:
                fill_hidden(ring - hop)
        if tick == 0:
            fetches["down"].wait()
            landed_all(down_second)
        if tick == max(LAG - 1, 0):
            landed_all(last_first)
            last_second = pass_down_second(1)
        if tick == LAG:
            landed_all(last_second)
        if tick < ring - 1:
            advance(0, tick)
            advance(1, tick)
        if tick >= LAG:
            advance(2, tick - LAG)
            advance(3, tick - LAG)
    for quarter in range(4):
        total = term(0, quarter)
        pending[quarter].wait_recv()
        total = (total + arriving[quarter, ring - 2].astype(f32)).astype(bf16)
        leaving[:, pl.ds(quarter * quarter_width, quarter_width)] = mul(spread, total).astype(bf16)
    back = [
        remote(
            leaving.at[pl.ds(j * PADDED, PADDED)],
            returned.at[pl.ds(j * PADDED, PADDED)],
            back_send.at[j],
            back_recv.at[j],
            peer(peers - j),
        )
        for j in range(1, peers)
    ]
    returned[pl.ds(0, PADDED)] = leaving[pl.ds(0, PADDED)]
    landed_all(back)

    combined = mul(weighted_high, returned[...]) + mul(weighted_low, returned[...])
    finished = (state + combined).astype(bf16)
    patch_out[...] = finished

    fetches["dkv"].wait()
    pairs = mul(finished, w_dkv[...]).astype(bf16).astype(f32)
    nothing = jnp.zeros((PAIR - slot_count, width), f32)

    def by_head(block):
        parts = []
        for h in range(HEADS):
            parts += [jnp.where(in_head(block.shape, h), block, 0.0), nothing]
        return jnp.concatenate(parts, axis=0).astype(bf16)

    scores = mul_over_last(byte_queries, by_head(pairs[:, :width]))
    allowed = iota((count, PAIR), 1).astype(f32) <= number_column
    weighed = []
    for h in range(HEADS):
        part = jnp.where(allowed, scores[:, h * PAIR : (h + 1) * PAIR], very_negative)
        raised = jnp.exp(part - jnp.max(part, axis=-1, keepdims=True))
        weighed.append((raised / jnp.sum(raised, axis=-1, keepdims=True)).astype(bf16))
    mixed = mul(jnp.concatenate(weighed, axis=1), by_head(pairs[:, width:])).astype(bf16)
    fetches["do"].wait()
    bytes_out[...] = (encoded.astype(f32) + mul(mixed, w_do[...])).astype(bf16)
    for copy in started:
        copy.wait_send()


def per_device(
    byte_states,
    patch_start,
    expert_ids,
    enc_gain,
    w_qkv,
    w_out,
    w_xq,
    w_xkv,
    w_up,
    moe_gain,
    w_router,
    w_in,
    w_down,
    dec_gain,
    w_dq,
    w_dkv,
    w_do,
):
    groups, ring, peers = (lax.axis_size(axis) for axis in SEQ_EXPERT)
    count, width = byte_states.shape
    slot_count = expert_ids.shape[0]
    outer = w_up.shape[1]
    share = w_down.shape[1]
    rows = peers * (12 * slot_count // (5 * peers))
    scaled = (w_up.astype(f32) * moe_gain).astype(bf16)
    folded = lax.dot_general(
        w_in[0], scaled, (((0,), (1,)), ((), ())), preferred_element_type=f32
    ).astype(bf16)
    dma = pltpu.SemaphoreType.DMA
    vmem = pltpu.VMEM
    weights = [w_qkv, w_out, w_xq, w_xkv, w_up, w_dq, w_dkv, w_do]
    return pl.pallas_call(
        functools.partial(step_kernel, (groups, ring, peers)),
        out_shape=(
            jax.ShapeDtypeStruct((count, width), bf16),
            jax.ShapeDtypeStruct((slot_count, outer), bf16),
        ),
        in_specs=[pl.BlockSpec(memory_space=pltpu.VMEM)] * 7
        + [pl.BlockSpec(memory_space=pl.ANY)] * 10,
        out_specs=(pl.BlockSpec(memory_space=pltpu.VMEM),) * 2,
        scratch_shapes=[vmem(w.shape, bf16) for w in weights]
        + [
            vmem((2, groups * share, width), bf16),
            vmem((groups * share, outer), bf16),
            vmem((2, count, width), bf16),
            vmem((3, count, width), bf16),
            vmem((3, count, width), bf16),
            vmem((count, width), bf16),
            vmem((peers * PADDED, width), bf16),
            vmem((peers * PADDED, width), bf16),
            vmem((ring, rows, width), bf16),
            vmem((ring, rows, groups * share), bf16),
            vmem((4, ring - 1, rows, outer // 4), bf16),
            vmem((4, ring - 1, rows, outer // 4), bf16),
            vmem((peers * PADDED, outer), bf16),
            vmem((peers * PADDED, outer), bf16),
            dma((10,)),
            dma((2,)),
            dma((2,)),
            dma((2, 6)),
            dma((2, 6)),
            dma((peers,)),
            dma((peers,)),
            dma((2, ring // 2 + 1)),
            dma((2, ring // 2 + 1)),
            dma((4, ring - 1)),
            dma((4, ring - 1)),
            dma((peers,)),
            dma((peers,)),
        ],
        compiler_params=pltpu.CompilerParams(
            collective_id=0, has_side_effects=True, vmem_limit_bytes=60 << 20
        ),
    )(
        byte_states,
        patch_start[None, :],
        expert_ids,
        enc_gain[None, :],
        moe_gain[None, :],
        dec_gain[None, :],
        w_router,
        folded,
        w_down[0],
        *weights,
    )


def solution(mesh):
    split = Mesh(mesh.devices.reshape(4, 8, mesh.shape["expert"]), SEQ_EXPERT)
    placed = (
        P(SEQ_EXPERT, None),
        P(SEQ_EXPERT),
        P(SEQ_EXPERT, None),
        P(),
        P(),
        P(),
        P(),
        P(),
        P(),
        P(),
        P(),
        P("expert", None, None, SEQ),
        P("expert", SEQ, None),
        P(),
        P(),
        P(),
        P(),
    )
    return jax.shard_map(
        per_device,
        mesh=split,
        in_specs=placed,
        out_specs=(P(SEQ_EXPERT, None), P(SEQ_EXPERT, None)),
        check_vma=False,
    )
```

time: 396 us -> 115 us (0.29)
  waiting for transfers between devices: 286 us -> 0 us
  Pallas kernels: 0 us -> 104 us
  matrix products: 41.2 us -> 2.64 us
  starting transfers between devices: 16.9 us -> 0 us
  between operations: 14.2 us -> 0.66 us
  blocking collectives: 12.9 us -> 0 us
  other arithmetic: 9.47 us -> 0.81 us
  local copies, waits for them, and re-layouts: 14.8 us -> 7.35 us
    reduce_scatter x2 -> x0, waiting for transfers between devices: 159 us -> none  [own_rows(): subtotal = lax.psum_scatter(subtotal, axis, scatter_dimension=0, tiled=True)]
    all_gather x1 -> x0, waiting for transfers between devices: 118 us -> none  [mixture(): lax.all_gather(rows, SEQ, axis=0, tiled=True)]
    pallas_call x0 -> x1, Pallas kernels: none -> 104 us  [per_device(): pl.pallas_call(functools.partial(step_kernel, (groups, ring, peers)), out...]
    dot_general x19 -> x0, matrix products: 35 us -> none  [the longest x1 8.58 us: mixture(): jnp.einsum('red,edk->rek', lax.all_gather(rows, SEQ, axis=0, tiled=True),...]
    all_to_all x1 -> x0, blocking collectives: 12.9 us -> none  [mixture(): lax.all_to_all(routed.reshape(expert_devices, capacity * local_experts, g...]
    all_to_all x1 -> x0, waiting for transfers between devices: 8.75 us -> none  [mixture(): lax.all_to_all(results, 'expert', split_axis=0, concat_axis=0, tiled=True)]
    ppermute x2 -> x0, starting transfers between devices: 8.48 us -> none  [passed_along(): return lax.ppermute(x, axis, pairs)]
    all_to_all x1 -> x0, starting transfers between devices: 8.13 us -> none  [mixture(): lax.all_to_all(results, 'expert', split_axis=0, concat_axis=0, tiled=True)]
  transfers between devices with their start and end apart: 6 -> 0, of which waited for: 4 -> 0; matrix products, arithmetic and copies ran while one was open for 3% -> 0% of each run, Pallas kernels for 0% -> 0%
where the time goes in v3:
time: 115 us
  Pallas kernels  104 us (90%)
  local copies, waits for them, and re-layouts  7.35 us (6%)
  matrix products  2.64 us (2%)
    pallas_call x1, Pallas kernels, per_device(): pl.pallas_call(functools.partial(step_kernel, (groups, ring, peers)), out...  104 us
    unnamed x8, local copies, waits for them, and re-layouts  7.35 us
    unnamed x1, matrix products  2.64 us

profile of v3, /device:TPU:1, one launch (start us, length us, event | category | flops | bytes accessed | tf_op | source)
XLA Modules:
  0.0 115.0 jit_solution(18034643555455414618)
XLA Ops:
  0.6 0.0 copy-start
  0.6 1.4 %copy-done = bf16[1,2048,2,192]{1,3,2,0:T(8,128)(2,1)S(1)} copy-done((bf16[1,2048,2,192]{1,3,2,0:T(8,128)(2,1)S(1)}, bf16[1,2048,2,192]{1,3,2,0:T(8,128)(2,1)}, u32[]{:S(2)}) %copy-start) | copy-done | bytes 1572888
  2.0 1.4 %copy.19.ids = s32[40,2]{1,0:T(8,128)} copy(s32[40,2]{0,1:T(2,128)} %param.19) | data formatting | bytes 640 | tf_op args[2]
  3.4 0.0 copy-start.1
  3.4 2.6 %fusion = f32[512,384]{0,1:S(1)} fusion(bf16[2048,384]{0,1:T(8,128)(2,1)S(1)} %bitcast.12, bf16[512,2048]{1,0:T(8,128)(2,1)} %w_up_hbm.1, f32[2048]{0:T(1024)} %param.26), kind=kOutput, calls=%fused_computation.1 | convolution fusion | flops 808452096 | bytes 4464640
  6.1 0.8 convert_bitcast_fusion.folded
  6.9 0.0 copy-done.1
  6.9 1.3 %copy.20.w_router = f32[2048,8]{1,0:T(8,128)} copy(f32[2048,8]{0,1:T(8,128)S(1)} %copy-done.1) | data formatting | bytes 131072 | tf_op args[10]
  8.2 103.5 %shard_map.176 = (bf16[256,512]{1,0:T(8,128)(2,1)}, bf16[40,2048]{1,0:T(8,128)(2,1)}) custom-call(bf16[256,512]{1,0:T(8,128)(2,1)} %states.1, s32[1,256]{1,0:T(1,128)} %bitcast.18, s32[40,2]{1,0:T(8,128)} %copy.19.ids, f32[1,512]{1,0:T(1,128)} %bitcast.16, f32[1,2048]{1,0:T(1,128)} %bitcast.15, f32[1,512]{1,0:T(1,128)} %bitcast.17, ...), custom_call_target="tpu_custom_call" | custom-call | tf_op jit(solution)/shard_map/pallas_call | solution.py:542
  111.7 1.7 %copy.23 = bf16[256,512]{1,0:T(8,128)(2,1)} copy(bf16[256,512]{1,0:T(8,128)(2,1)} %get-tuple-element.4) | data formatting | bytes 524288
  113.4 1.6 %copy.24 = bf16[40,2048]{1,0:T(8,128)(2,1)} copy(bf16[40,2048]{1,0:T(8,128)(2,1)} %get-tuple-element.5) | data formatting | bytes 327680
Async XLA Ops:
  0.6 1.4 %copy-start = (bf16[1,2048,2,192]{1,3,2,0:T(8,128)(2,1)S(1)}, bf16[1,2048,2,192]{1,3,2,0:T(8,128)(2,1)}, u32[]{:S(2)}) copy-start(bf16[1,2048,2,192]{1,3,2,0:T(8,128)(2,1)} %param.28) | copy-start | bytes 4718596
  3.4 3.5 %copy-start.1 = (f32[2048,8]{0,1:T(8,128)S(1)}, f32[2048,8]{0,1:T(8,128)}, u32[]{:S(2)}) copy-start(f32[2048,8]{0,1:T(8,128)} %param.27) | copy-start | bytes 196612

commit v4 on v3

--- a/solution.py
+++ b/solution.py
@@ -50,14 +50,14 @@
 
 def step_kernel(
     sizes,
-    states,
-    flags,
-    ids,
-    enc_gain,
-    moe_gain,
-    dec_gain,
-    w_router,
-    folded,
+    states_hbm,
+    flags_hbm,
+    ids_hbm,
+    enc_gain_hbm,
+    moe_gain_hbm,
+    dec_gain_hbm,
+    w_router_hbm,
+    w_in_hbm,
     w_down,
     w_qkv_hbm,
     w_out_hbm,
@@ -69,6 +69,14 @@
     w_do_hbm,
     bytes_out,
     patch_out,
+    states,
+    flags,
+    ids,
+    enc_gain,
+    moe_gain,
+    dec_gain,
+    w_router,
+    w_in,
     w_qkv,
     w_out,
     w_xq,
@@ -116,7 +124,7 @@
     down = {"seq_0": lax.rem(plane + groups - 1, groups)}
     count, width = states.shape
     slot_count, outer = patch_out.shape
-    share = folded.shape[1]
+    share = w_down.shape[0]
     capacity = slots.shape[1] // peers
     rows = peers * capacity
     quarter_width = outer // 4
@@ -143,12 +151,19 @@
     fetches = {}
     for number, (name, source, target) in enumerate(
         [
+            ("states", states_hbm, states),
+            ("moe_gain", moe_gain_hbm, moe_gain),
+            ("w_in", w_in_hbm, w_in),
+            ("w_up", w_up_hbm, w_up),
+            ("enc_gain", enc_gain_hbm, enc_gain),
             ("qkv", w_qkv_hbm, w_qkv),
+            ("flags", flags_hbm, flags),
+            ("ids", ids_hbm, ids),
             ("out", w_out_hbm, w_out),
             ("xkv", w_xkv_hbm, w_xkv),
             ("xq", w_xq_hbm, w_xq),
-            ("w_up", w_up_hbm, w_up),
-            ("up", folded, up_held.at[:, pl.ds(0, share)]),
+            ("router", w_router_hbm, w_router),
+            ("dec_gain", dec_gain_hbm, dec_gain),
             ("down", w_down, down_held.at[pl.ds(0, share)]),
             ("dq", w_dq_hbm, w_dq),
             ("dkv", w_dkv_hbm, w_dkv),
@@ -156,7 +171,10 @@
         ]
     ):
         fetches[name] = pltpu.make_async_copy(source, target, fetch_sem.at[number])
-        fetches[name].start()
+    late = ("down", "dq", "dkv", "do")
+    for name in fetches:
+        if name not in late:
+            fetches[name].start()
     pl.semaphore_wait(barrier, len(partners))
 
     started = []
@@ -174,8 +192,8 @@
         started.append(copy)
         return copy
 
-    near = remote(states, halo.at[1], halo_send.at[0], halo_recv.at[0], stretch(1))
-    far = remote(states, halo.at[0], halo_send.at[1], halo_recv.at[1], stretch(2))
+    near = remote(states_hbm, halo.at[1], halo_send.at[0], halo_recv.at[0], stretch(1))
+    far = remote(states_hbm, halo.at[0], halo_send.at[1], halo_recv.at[1], stretch(2))
 
     def weight_copy(stage, direction, source, target):
         return remote(
@@ -196,7 +214,7 @@
         ]
 
     def pass_up_first():
-        return [weight_copy(0, d, folded, up_slice((1, 3)[d])) for d in range(2)]
+        return [weight_copy(0, d, up_slice(0), up_slice((1, 3)[d])) for d in range(2)]
 
     def pass_up_second():
         copies = []
@@ -226,15 +244,22 @@
         for copy in copies:
             copy.wait_recv()
 
+    down_first = pass_down_first(0)
+    for name in ("moe_gain", "w_in", "w_up"):
+        fetches[name].wait()
+    scaled = (w_in[...].astype(f32) * moe_gain[...]).astype(bf16)
+    folded = mul_over_last(scaled, w_up[...]).astype(bf16)
+    up_held[0, pl.ds(0, share)] = folded[:share]
+    up_held[1, pl.ds(0, share)] = folded[share:]
     up_first = pass_up_first()
-    down_first = pass_down_first(0)
 
     def keep_pairs(number, projected):
         kept = projected.astype(bf16)
         keys[number] = kept[:, :width]
         values[number] = kept[:, width:]
 
-    fetches["qkv"].wait()
+    for name in ("states", "enc_gain", "qkv"):
+        fetches[name].wait()
     normed = rms_scale(states[...], enc_gain[...]).astype(bf16)
     queries = (mul(normed, w_qkv[:, pl.ds(0, width)]).astype(bf16).astype(f32) * 0.125).astype(bf16)
     keep_pairs(2, mul(normed, w_qkv[:, pl.ds(width, 2 * width)]))
@@ -276,11 +301,14 @@
             outs.append(mixed / total)
         mixing[:, columns] = jnp.where(first_half, outs[0], outs[1]).astype(bf16)
         if pair == 1:
-            landed_all(up_first)
-            up_second = pass_up_second()
+            landed_all(down_first)
+            down_second = pass_down_second(0)
     fetches["out"].wait()
+    for name in late:
+        fetches[name].start()
     encoded = (states[...].astype(f32) + mul(mixing[...], w_out[...])).astype(bf16)
 
+    fetches["flags"].wait()
     opened = flags[...].astype(f32)
     row_at = iota((count, count), 0)
     column_at = iota((count, count), 1)
@@ -319,12 +347,17 @@
         part = spread_out[h * slot_count : (h + 1) * slot_count]
         patch_mix = patch_mix + jnp.where(in_head(part.shape, h), part, 0.0)
     patch_input = jnp.where(live > 0.5, patch_mix, 0.0).astype(bf16)
-    fetches["w_up"].wait()
     state = mul(patch_input, w_up[...]).astype(bf16).astype(f32)
     scale = lax.rsqrt(jnp.mean(state * state, axis=-1, keepdims=True) + epsilon)
 
     lane = iota((slot_count, peers * PADDED), 1)
-    expert = [ids[:, k : k + 1] for k in range(2)]
+    fetches["ids"].wait()
+    same = iota((slot_count,) * 2, 0) == iota((slot_count,) * 2, 1)
+    ids_row = [ids[k : k + 1].astype(f32) for k in range(2)]
+    expert = [
+        jnp.sum(jnp.where(same, row, 0.0), axis=1, keepdims=True).astype(jnp.int32)
+        for row in ids_row
+    ]
     named = [jnp.where(lane == expert[k], 1.0, 0.0) for k in range(2)]
     before = jnp.where(iota((slot_count,) * 2, 1) < iota((slot_count,) * 2, 0), 1.0, 0.0)
     counted = mul(before.astype(bf16), (named[0] + named[1]).astype(bf16))
@@ -349,14 +382,13 @@
         for j in range(1, peers)
     ]
     landed[pl.ds(0, PADDED)] = routed[pl.ds(0, PADDED)]
-    landed_all(down_first)
-    down_second = pass_down_second(0)
-    last_first = pass_down_first(1)
 
     patch_normed = (state * scale * moe_gain[...]).astype(bf16)
-    logits = jnp.dot(
+    fetches["router"].wait()
+    logits = lax.dot_general(
         patch_normed.astype(f32),
         w_router[...],
+        (((1,), (1,)), ((), ())),
         precision=lax.Precision.HIGHEST,
         preferred_element_type=f32,
     )
@@ -374,6 +406,7 @@
     weighted_high = weighted.astype(bf16)
     weighted_low = (weighted - weighted_high.astype(f32)).astype(bf16)
     fetches["dq"].wait()
+    fetches["dec_gain"].wait()
     byte_normed = rms_scale(encoded, dec_gain[...]).astype(bf16)
     byte_queries = (mul(byte_normed, w_dq[...]).astype(bf16).astype(f32) * 0.125).astype(bf16)
 
@@ -434,8 +467,34 @@
             right if quarter % 2 == 0 else left,
         )
 
+    def send_back(part):
+        columns = pl.ds(part * (outer // 2), outer // 2)
+        for quarter in (2 * part, 2 * part + 1):
+            total = term(0, quarter)
+            pending[quarter].wait_recv()
+            total = (total + arriving[quarter, ring - 2].astype(f32)).astype(bf16)
+            leaving[:, pl.ds(quarter * quarter_width, quarter_width)] = mul(
+                spread, total
+            ).astype(bf16)
+        copies = []
+        for j in range(1, peers):
+            rows_of = pl.ds(j * PADDED, PADDED)
+            copies.append(
+                remote(
+                    leaving.at[rows_of, columns],
+                    returned.at[rows_of, columns],
+                    back_send.at[part, j],
+                    back_recv.at[part, j],
+                    peer(peers - j),
+                )
+            )
+        returned[pl.ds(0, PADDED), columns] = leaving[pl.ds(0, PADDED), columns]
+        return copies
+
     to_right, to_left = forward_right(1), forward_left(1)
-    fetches["up"].wait()
+    landed_all(up_first)
+    up_second = pass_up_second()
+    last_first = pass_down_first(1)
     landed_all(up_second)
     fill_hidden(0)
     for tick in range(ring - 1 + LAG):
@@ -461,30 +520,25 @@
         if tick >= LAG:
             advance(2, tick - LAG)
             advance(3, tick - LAG)
-    for quarter in range(4):
-        total = term(0, quarter)
-        pending[quarter].wait_recv()
-        total = (total + arriving[quarter, ring - 2].astype(f32)).astype(bf16)
-        leaving[:, pl.ds(quarter * quarter_width, quarter_width)] = mul(spread, total).astype(bf16)
-    back = [
-        remote(
-            leaving.at[pl.ds(j * PADDED, PADDED)],
-            returned.at[pl.ds(j * PADDED, PADDED)],
-            back_send.at[j],
-            back_recv.at[j],
-            peer(peers - j),
+        if tick == ring - 1:
+            back = [send_back(0)]
+    if LAG == 0:
+        back = [send_back(0)]
+    back.append(send_back(1))
+
+    fetches["dkv"].wait()
+    pairs = 0.0
+    for part in range(2):
+        columns = pl.ds(part * (outer // 2), outer // 2)
+        landed_all(back[part])
+        combined = mul(weighted_high, returned[:, columns]) + mul(
+            weighted_low, returned[:, columns]
         )
-        for j in range(1, peers)
-    ]
-    returned[pl.ds(0, PADDED)] = leaving[pl.ds(0, PADDED)]
-    landed_all(back)
-
-    combined = mul(weighted_high, returned[...]) + mul(weighted_low, returned[...])
-    finished = (state + combined).astype(bf16)
-    patch_out[...] = finished
-
-    fetches["dkv"].wait()
-    pairs = mul(finished, w_dkv[...]).astype(bf16).astype(f32)
+        finished = state[:, part * (outer // 2) : (part + 1) * (outer // 2)] + combined
+        patch_out[:, columns] = finished
+        pairs = pairs + mul(finished.astype(bf16), w_dkv[columns])
+
+    pairs = pairs.astype(bf16).astype(f32)
     nothing = jnp.zeros((PAIR - slot_count, width), f32)
 
     def by_head(block):
@@ -502,7 +556,7 @@
         weighed.append((raised / jnp.sum(raised, axis=-1, keepdims=True)).astype(bf16))
     mixed = mul(jnp.concatenate(weighed, axis=1), by_head(pairs[:, width:])).astype(bf16)
     fetches["do"].wait()
-    bytes_out[...] = (encoded.astype(f32) + mul(mixed, w_do[...])).astype(bf16)
+    bytes_out[...] = encoded.astype(f32) + mul(mixed, w_do[...])
     for copy in started:
         copy.wait_send()
 
@@ -532,23 +586,28 @@
     outer = w_up.shape[1]
     share = w_down.shape[1]
     rows = peers * (12 * slot_count // (5 * peers))
-    scaled = (w_up.astype(f32) * moe_gain).astype(bf16)
-    folded = lax.dot_general(
-        w_in[0], scaled, (((0,), (1,)), ((), ())), preferred_element_type=f32
-    ).astype(bf16)
     dma = pltpu.SemaphoreType.DMA
     vmem = pltpu.VMEM
+    small = [
+        byte_states,
+        patch_start[None, :],
+        expert_ids.T,
+        enc_gain[None, :],
+        moe_gain[None, :],
+        dec_gain[None, :],
+        w_router.T,
+        jnp.transpose(w_in[0], (1, 2, 0)).reshape(2 * share, outer),
+    ]
     weights = [w_qkv, w_out, w_xq, w_xkv, w_up, w_dq, w_dkv, w_do]
-    return pl.pallas_call(
+    made = pl.pallas_call(
         functools.partial(step_kernel, (groups, ring, peers)),
         out_shape=(
-            jax.ShapeDtypeStruct((count, width), bf16),
-            jax.ShapeDtypeStruct((slot_count, outer), bf16),
+            jax.ShapeDtypeStruct((count, width), f32),
+            jax.ShapeDtypeStruct((slot_count, outer), f32),
         ),
-        in_specs=[pl.BlockSpec(memory_space=pltpu.VMEM)] * 7
-        + [pl.BlockSpec(memory_space=pl.ANY)] * 10,
+        in_specs=[pl.BlockSpec(memory_space=pl.ANY)] * 17,
         out_specs=(pl.BlockSpec(memory_space=pltpu.VMEM),) * 2,
-        scratch_shapes=[vmem(w.shape, bf16) for w in weights]
+        scratch_shapes=[vmem(w.shape, w.dtype) for w in small + weights]
         + [
             vmem((2, groups * share, width), bf16),
             vmem((groups * share, outer), bf16),
@@ -564,7 +623,7 @@
             vmem((4, ring - 1, rows, outer // 4), bf16),
             vmem((peers * PADDED, outer), bf16),
             vmem((peers * PADDED, outer), bf16),
-            dma((10,)),
+            dma((17,)),
             dma((2,)),
             dma((2,)),
             dma((2, 6)),
@@ -575,24 +634,14 @@
             dma((2, ring // 2 + 1)),
             dma((4, ring - 1)),
             dma((4, ring - 1)),
-            dma((peers,)),
-            dma((peers,)),
+            dma((2, peers)),
+            dma((2, peers)),
         ],
         compiler_params=pltpu.CompilerParams(
-            collective_id=0, has_side_effects=True, vmem_limit_bytes=60 << 20
+            collective_id=0, has_side_effects=True, vmem_limit_bytes=64000000
         ),
-    )(
-        byte_states,
-        patch_start[None, :],
-        expert_ids,
-        enc_gain[None, :],
-        moe_gain[None, :],
-        dec_gain[None, :],
-        w_router,
-        folded,
-        w_down[0],
-        *weights,
-    )
+    )(*small, w_down[0], *weights)
+    return tuple(value.astype(bf16) for value in made)
 
 
 def solution(mesh):

time: 115 us -> 110 us (0.957)
  local copies, waits for them, and re-layouts: 7.35 us -> 0 us
  matrix products: 2.64 us -> 0 us
  other arithmetic: 0.81 us -> 3.43 us
  Pallas kernels: 104 us -> 106 us
    unnamed x8 -> x0, local copies, waits for them, and re-layouts: 7.35 us -> none
    unnamed x1 -> x0, matrix products: 2.64 us -> none
    convert_element_type x1 -> x2, other arithmetic: 0.81 us -> 3.43 us  [per_device(): return tuple((value.astype(bf16) for value in made))]
    pallas_call x1, Pallas kernels: 104 us -> 106 us  [per_device(): pl.pallas_call(functools.partial(step_kernel, (groups, ring, peers)), out...]
where the time goes in v4:
time: 110 us
  Pallas kernels  106 us (96%)
  other arithmetic  3.43 us (3%)
    pallas_call x1, Pallas kernels, per_device(): pl.pallas_call(functools.partial(step_kernel, (groups, ring, peers)), out...  106 us
    convert_element_type x2, other arithmetic, per_device(): return tuple((value.astype(bf16) for value in made))  3.43 us

profile of v4, /device:TPU:1, one launch (start us, length us, event | category | flops | bytes accessed | tf_op | source)
XLA Modules:
  0.0 109.7 jit_solution(10395054131998405639)
XLA Ops:
  0.6 105.6 %shard_map.176 = (f32[256,512]{1,0:T(8,128)}, f32[40,2048]{1,0:T(8,128)}) custom-call(bf16[256,512]{1,0:T(8,128)(2,1)} %states_hbm.1, s32[1,256]{1,0:T(1,128)} %bitcast.18, s32[2,40]{1,0:T(2,128)} %bitcast.19, f32[1,512]{1,0:T(1,128)} %bitcast.16, f32[1,2048]{1,0:T(1,128)} %bitcast.15, f32[1,512]{1,0:T(1,128)} %bitcast.17, f32[8,2048]{1,0:T(8,128)} %bitcast.14, ...), custom_call_target="tpu_custom_call" | custom-call | tf_op jit(solution)/shard_map/pallas_call | solution.py:602
  106.3 1.8 %convert_element_type.6 = bf16[256,512]{1,0:T(8,128)(2,1)} convert(f32[256,512]{1,0:T(8,128)} %get-tuple-element.4) | non-fusion elementwise | flops 131072 | bytes 786432 | tf_op jit(solution)/shard_map/convert_element_type | solution.py:644
  108.1 1.7 %convert_element_type.7 = bf16[40,2048]{1,0:T(8,128)(2,1)} convert(f32[40,2048]{1,0:T(8,128)} %get-tuple-element.5) | non-fusion elementwise | flops 81920 | bytes 491520 | tf_op jit(solution)/shard_map/convert_element_type | solution.py:644

commit v5 on v4

--- a/solution.py
+++ b/solution.py
@@ -12,7 +12,9 @@
 HEAD = 64
 PAIR = 2 * HEAD
 PADDED = 16
-LAG = 3
+PARTS = (1024, 1024)
+LAGS = (0, 2)
+PIECES = 2
 SEQ = ("seq_0", "seq_1")
 SEQ_EXPERT = ("seq_0", "seq_1", "expert")
 
@@ -86,7 +88,8 @@
     w_dkv,
     w_do,
     up_held,
-    down_held,
+    down_0,
+    down_1,
     halo,
     keys,
     values,
@@ -95,8 +98,10 @@
     landed,
     slots,
     hidden,
-    sending,
-    arriving,
+    sending_0,
+    sending_1,
+    arriving_0,
+    arriving_1,
     leaving,
     returned,
     fetch_sem,
@@ -127,7 +132,10 @@
     share = w_down.shape[0]
     capacity = slots.shape[1] // peers
     rows = peers * capacity
-    quarter_width = outer // 4
+    down_held = (down_0, down_1)
+    sending = (sending_0, sending_1)
+    arriving = (arriving_0, arriving_1)
+    bases = [sum(PARTS[:part]) for part in range(len(PARTS))]
     half = ring // 2
 
     def peer(j):
@@ -151,6 +159,7 @@
     fetches = {}
     for number, (name, source, target) in enumerate(
         [
+            ("down_0", w_down.at[:, pl.ds(0, PARTS[0])], down_0.at[pl.ds(0, share)]),
             ("states", states_hbm, states),
             ("moe_gain", moe_gain_hbm, moe_gain),
             ("w_in", w_in_hbm, w_in),
@@ -164,14 +173,14 @@
             ("xq", w_xq_hbm, w_xq),
             ("router", w_router_hbm, w_router),
             ("dec_gain", dec_gain_hbm, dec_gain),
-            ("down", w_down, down_held.at[pl.ds(0, share)]),
+            ("down_1", w_down.at[:, pl.ds(PARTS[0], PARTS[1])], down_1.at[pl.ds(0, share)]),
             ("dq", w_dq_hbm, w_dq),
             ("dkv", w_dkv_hbm, w_dkv),
             ("do", w_do_hbm, w_do),
         ]
     ):
         fetches[name] = pltpu.make_async_copy(source, target, fetch_sem.at[number])
-    late = ("down", "dq", "dkv", "do")
+    late = ("dq", "dkv", "do")
     for name in fetches:
         if name not in late:
             fetches[name].start()
@@ -208,10 +217,7 @@
         return up_held.at[:, pl.ds(slot * share, share)]
 
     def down_slice(slot, part, rows_from=0, rows_count=None):
-        return down_held.at[
-            pl.ds(slot * share + rows_from, rows_count or share),
-            pl.ds(part * (outer // 2), outer // 2),
-        ]
+        return down_held[part].at[pl.ds(slot * share + rows_from, rows_count or share)]
 
     def pass_up_first():
         return [weight_copy(0, d, up_slice(0), up_slice((1, 3)[d])) for d in range(2)]
@@ -224,7 +230,7 @@
         return copies
 
     def pass_down_first(part):
-        source = w_down.at[:, pl.ds(part * (outer // 2), outer // 2)]
+        source = down_slice(0, part)
         return [
             weight_copy(2 + 2 * part, d, source, down_slice((1, 3)[d], part)) for d in range(2)
         ]
@@ -244,6 +250,7 @@
         for copy in copies:
             copy.wait_recv()
 
+    fetches["down_0"].wait()
     down_first = pass_down_first(0)
     for name in ("moe_gain", "w_in", "w_up"):
         fetches[name].wait()
@@ -448,34 +455,43 @@
         upper = mul_over_last(block, up_held[1])
         hidden[slot] = (gate / (1.0 + jnp.exp(-gate)) * upper).astype(bf16)
 
-    def term(slot, quarter):
-        return mul(hidden[slot], down_held[:, pl.ds(quarter * quarter_width, quarter_width)])
-
-    pending = [None] * 4
-
-    def advance(quarter, step):
-        total = term(step + 1 if quarter % 2 == 0 else ring - 1 - step, quarter)
-        if step > 0:
-            pending[quarter].wait_recv()
-            total = total + arriving[quarter, step - 1].astype(f32)
-        sending[quarter, step] = total.astype(bf16)
-        pending[quarter] = remote(
-            sending.at[quarter, step],
-            arriving.at[quarter, step],
-            ring_send.at[quarter, step],
-            ring_recv.at[quarter, step],
-            right if quarter % 2 == 0 else left,
-        )
+    def ring_columns(part, direction):
+        return pl.ds(bases[part] + direction * (PARTS[part] // 2), PARTS[part] // 2)
+
+    def term(slot, part, direction):
+        columns = pl.ds(direction * (PARTS[part] // 2), PARTS[part] // 2)
+        return mul(hidden[slot], down_held[part][:, columns])
+
+    pending = {}
+
+    def advance(part, step):
+        for direction in range(2):
+            total = term(step + 1 if direction == 0 else ring - 1 - step, part, direction)
+            for piece in range(PIECES):
+                begin = piece * (rows // PIECES)
+                piece_rows = pl.ds(begin, rows // PIECES)
+                value = total[begin : begin + rows // PIECES]
+                if step > 0:
+                    pending[part, direction, piece].wait_recv()
+                    value = value + arriving[part][direction, step - 1, piece_rows].astype(f32)
+                sending[part][direction, step, piece_rows] = value.astype(bf16)
+                number = (part * 2 + direction) * PIECES + piece
+                pending[part, direction, piece] = remote(
+                    sending[part].at[direction, step, piece_rows],
+                    arriving[part].at[direction, step, piece_rows],
+                    ring_send.at[number, step],
+                    ring_recv.at[number, step],
+                    right if direction == 0 else left,
+                )
 
     def send_back(part):
-        columns = pl.ds(part * (outer // 2), outer // 2)
-        for quarter in (2 * part, 2 * part + 1):
-            total = term(0, quarter)
-            pending[quarter].wait_recv()
-            total = (total + arriving[quarter, ring - 2].astype(f32)).astype(bf16)
-            leaving[:, pl.ds(quarter * quarter_width, quarter_width)] = mul(
-                spread, total
-            ).astype(bf16)
+        columns = pl.ds(bases[part], PARTS[part])
+        for direction in range(2):
+            total = term(0, part, direction)
+            for piece in range(PIECES):
+                pending[part, direction, piece].wait_recv()
+            total = (total + arriving[part][direction, ring - 2].astype(f32)).astype(bf16)
+            leaving[:, ring_columns(part, direction)] = mul(spread, total).astype(bf16)
         copies = []
         for j in range(1, peers):
             rows_of = pl.ds(j * PADDED, PADDED)
@@ -494,10 +510,12 @@
     to_right, to_left = forward_right(1), forward_left(1)
     landed_all(up_first)
     up_second = pass_up_second()
-    last_first = pass_down_first(1)
+    fetches["down_1"].wait()
+    down_first = pass_down_first(1)
     landed_all(up_second)
     fill_hidden(0)
-    for tick in range(ring - 1 + LAG):
+    back = []
+    for tick in range(LAGS[-1] + ring):
         hop = tick + 1
         if hop <= half:
             landed_all([to_right, to_left])
@@ -506,35 +524,30 @@
             fill_hidden(hop)
             if hop < half:
                 fill_hidden(ring - hop)
-        if tick == 0:
-            fetches["down"].wait()
+        if tick in LAGS:
             landed_all(down_second)
-        if tick == max(LAG - 1, 0):
-            landed_all(last_first)
-            last_second = pass_down_second(1)
-        if tick == LAG:
-            landed_all(last_second)
-        if tick < ring - 1:
-            advance(0, tick)
-            advance(1, tick)
-        if tick >= LAG:
-            advance(2, tick - LAG)
-            advance(3, tick - LAG)
-        if tick == ring - 1:
-            back = [send_back(0)]
-    if LAG == 0:
-        back = [send_back(0)]
-    back.append(send_back(1))
+        if tick + 1 in LAGS:
+            part = LAGS.index(tick + 1)
+            landed_all(down_first)
+            down_second = pass_down_second(part)
+            if part + 1 < len(PARTS):
+                down_first = pass_down_first(part + 1)
+        for part in range(len(PARTS)):
+            step = tick - LAGS[part]
+            if 0 <= step < ring - 1:
+                advance(part, step)
+            if step == ring - 1:
+                back.append(send_back(part))
 
     fetches["dkv"].wait()
     pairs = 0.0
-    for part in range(2):
-        columns = pl.ds(part * (outer // 2), outer // 2)
+    for part in range(len(PARTS)):
+        columns = pl.ds(bases[part], PARTS[part])
         landed_all(back[part])
         combined = mul(weighted_high, returned[:, columns]) + mul(
             weighted_low, returned[:, columns]
         )
-        finished = state[:, part * (outer // 2) : (part + 1) * (outer // 2)] + combined
+        finished = state[:, bases[part] : bases[part] + PARTS[part]] + combined
         patch_out[:, columns] = finished
         pairs = pairs + mul(finished.astype(bf16), w_dkv[columns])
 
@@ -610,7 +623,7 @@
         scratch_shapes=[vmem(w.shape, w.dtype) for w in small + weights]
         + [
             vmem((2, groups * share, width), bf16),
-            vmem((groups * share, outer), bf16),
+            *[vmem((groups * share, part), bf16) for part in PARTS],
             vmem((2, count, width), bf16),
             vmem((3, count, width), bf16),
             vmem((3, count, width), bf16),
@@ -619,23 +632,22 @@
             vmem((peers * PADDED, width), bf16),
             vmem((ring, rows, width), bf16),
             vmem((ring, rows, groups * share), bf16),
-            vmem((4, ring - 1, rows, outer // 4), bf16),
-            vmem((4, ring - 1, rows, outer // 4), bf16),
+            *[vmem((2, ring - 1, rows, part // 2), bf16) for part in PARTS * 2],
             vmem((peers * PADDED, outer), bf16),
             vmem((peers * PADDED, outer), bf16),
-            dma((17,)),
+            dma((18,)),
             dma((2,)),
             dma((2,)),
-            dma((2, 6)),
-            dma((2, 6)),
+            dma((2, 2 + 2 * len(PARTS))),
+            dma((2, 2 + 2 * len(PARTS))),
             dma((peers,)),
             dma((peers,)),
             dma((2, ring // 2 + 1)),
             dma((2, ring // 2 + 1)),
-            dma((4, ring - 1)),
-            dma((4, ring - 1)),
-            dma((2, peers)),
-            dma((2, peers)),
+            dma((2 * PIECES * len(PARTS), ring - 1)),
+            dma((2 * PIECES * len(PARTS), ring - 1)),
+            dma((len(PARTS), peers)),
+            dma((len(PARTS), peers)),
         ],
         compiler_params=pltpu.CompilerParams(
             collective_id=0, has_side_effects=True, vmem_limit_bytes=64000000

time: 110 us -> 105 us (0.955)
  Pallas kernels: 106 us -> 101 us
    pallas_call x1, Pallas kernels: 106 us -> 101 us  [per_device(): pl.pallas_call(functools.partial(step_kernel, (groups, ring, peers)), out...]
where the time goes in v5:
time: 105 us
  Pallas kernels  101 us (96%)
  other arithmetic  3.43 us (3%)
    pallas_call x1, Pallas kernels, per_device(): pl.pallas_call(functools.partial(step_kernel, (groups, ring, peers)), out...  101 us
    convert_element_type x2, other arithmetic, per_device(): return tuple((value.astype(bf16) for value in made))  3.43 us

profile of v5, /device:TPU:1, one launch (start us, length us, event | category | flops | bytes accessed | tf_op | source)
XLA Modules:
  0.0 104.6 jit_solution(7824412697120464880)
XLA Ops:
  0.6 100.5 %shard_map.176 = (f32[256,512]{1,0:T(8,128)}, f32[40,2048]{1,0:T(8,128)}) custom-call(bf16[256,512]{1,0:T(8,128)(2,1)} %states_hbm.1, s32[1,256]{1,0:T(1,128)} %bitcast.18, s32[2,40]{1,0:T(2,128)} %bitcast.19, f32[1,512]{1,0:T(1,128)} %bitcast.16, f32[1,2048]{1,0:T(1,128)} %bitcast.15, f32[1,512]{1,0:T(1,128)} %bitcast.17, f32[8,2048]{1,0:T(8,128)} %bitcast.14, ...), custom_call_target="tpu_custom_call" | custom-call | tf_op jit(solution)/shard_map/pallas_call | solution.py:615
  101.2 1.8 %convert_element_type.6 = bf16[256,512]{1,0:T(8,128)(2,1)} convert(f32[256,512]{1,0:T(8,128)} %get-tuple-element.4) | non-fusion elementwise | flops 131072 | bytes 786432 | tf_op jit(solution)/shard_map/convert_element_type | solution.py:656
  102.9 1.7 %convert_element_type.7 = bf16[40,2048]{1,0:T(8,128)(2,1)} convert(f32[40,2048]{1,0:T(8,128)} %get-tuple-element.5) | non-fusion elementwise | flops 81920 | bytes 491520 | tf_op jit(solution)/shard_map/convert_element_type | solution.py:656

commit v6 on v5

--- a/solution.py
+++ b/solution.py
@@ -15,6 +15,7 @@
 PARTS = (1024, 1024)
 LAGS = (0, 2)
 PIECES = 2
+PASS_AT = 1
 SEQ = ("seq_0", "seq_1")
 SEQ_EXPERT = ("seq_0", "seq_1", "expert")
 
@@ -390,6 +391,11 @@
     ]
     landed[pl.ds(0, PADDED)] = routed[pl.ds(0, PADDED)]
 
+    landed_all(up_first)
+    up_second = pass_up_second()
+    fetches["down_1"].wait()
+    down_first = pass_down_first(1)
+
     patch_normed = (state * scale * moe_gain[...]).astype(bf16)
     fetches["router"].wait()
     logits = lax.dot_general(
@@ -508,10 +514,6 @@
         return copies
 
     to_right, to_left = forward_right(1), forward_left(1)
-    landed_all(up_first)
-    up_second = pass_up_second()
-    fetches["down_1"].wait()
-    down_first = pass_down_first(1)
     landed_all(up_second)
     fill_hidden(0)
     back = []
@@ -526,12 +528,9 @@
                 fill_hidden(ring - hop)
         if tick in LAGS:
             landed_all(down_second)
-        if tick + 1 in LAGS:
-            part = LAGS.index(tick + 1)
+        if tick == PASS_AT:
             landed_all(down_first)
-            down_second = pass_down_second(part)
-            if part + 1 < len(PARTS):
-                down_first = pass_down_first(part + 1)
+            down_second = pass_down_second(1)
         for part in range(len(PARTS)):
             step = tick - LAGS[part]
             if 0 <= step < ring - 1:
@@ -548,8 +547,9 @@
             weighted_low, returned[:, columns]
         )
         finished = state[:, bases[part] : bases[part] + PARTS[part]] + combined
+        finished = finished.astype(bf16)
         patch_out[:, columns] = finished
-        pairs = pairs + mul(finished.astype(bf16), w_dkv[columns])
+        pairs = pairs + mul(finished, w_dkv[columns])
 
     pairs = pairs.astype(bf16).astype(f32)
     nothing = jnp.zeros((PAIR - slot_count, width), f32)
@@ -569,9 +569,14 @@
         weighed.append((raised / jnp.sum(raised, axis=-1, keepdims=True)).astype(bf16))
     mixed = mul(jnp.concatenate(weighed, axis=1), by_head(pairs[:, width:])).astype(bf16)
     fetches["do"].wait()
-    bytes_out[...] = encoded.astype(f32) + mul(mixed, w_do[...])
+    bytes_out[...] = (encoded.astype(f32) + mul(mixed, w_do[...])).astype(bf16)
     for copy in started:
         copy.wait_send()
+
+
+def hand_over(bytes_in, patches_in, bytes_out, patches_out):
+    bytes_out[...] = bytes_in[...]
+    patches_out[...] = patches_in[...]
 
 
 def per_device(
@@ -615,8 +620,8 @@
     made = pl.pallas_call(
         functools.partial(step_kernel, (groups, ring, peers)),
         out_shape=(
-            jax.ShapeDtypeStruct((count, width), f32),
-            jax.ShapeDtypeStruct((slot_count, outer), f32),
+            jax.ShapeDtypeStruct((count, width), bf16),
+            jax.ShapeDtypeStruct((slot_count, outer), bf16),
         ),
         in_specs=[pl.BlockSpec(memory_space=pl.ANY)] * 17,
         out_specs=(pl.BlockSpec(memory_space=pltpu.VMEM),) * 2,
@@ -653,7 +658,12 @@
             collective_id=0, has_side_effects=True, vmem_limit_bytes=64000000
         ),
     )(*small, w_down[0], *weights)
-    return tuple(value.astype(bf16) for value in made)
+    return pl.pallas_call(
+        hand_over,
+        out_shape=tuple(jax.ShapeDtypeStruct(value.shape, bf16) for value in made),
+        in_specs=[pl.BlockSpec(memory_space=pltpu.VMEM)] * 2,
+        out_specs=(pl.BlockSpec(memory_space=pltpu.VMEM),) * 2,
+    )(*made)
 
 
 def solution(mesh):

time: 105 us -> 101 us (0.962)
  other arithmetic: 3.43 us -> 0 us
    convert_element_type x2 -> x0, other arithmetic: 3.43 us -> none  [per_device(): return tuple((value.astype(bf16) for value in made))]
    pallas_call x1, Pallas kernels: 101 us -> 98.7 us  [per_device(): pl.pallas_call(functools.partial(step_kernel, (groups, ring, peers)), out...]
    pallas_call x0 -> x1, Pallas kernels: none -> 1.77 us  [per_device(): pl.pallas_call(hand_over, out_shape=tuple((jax.ShapeDtypeStruct(value.sha...]
where the time goes in v6:
time: 101 us
  Pallas kernels  100 us (99%)
    pallas_call x1, Pallas kernels, per_device(): pl.pallas_call(functools.partial(step_kernel, (groups, ring, peers)), out...  98.7 us

profile of v6, /device:TPU:1, one launch (start us, length us, event | category | flops | bytes accessed | tf_op | source)
XLA Modules:
  0.0 101.1 jit_solution(1883814890477493173)
XLA Ops:
  0.6 98.7 %shard_map.176 = (bf16[256,512]{1,0:T(8,128)(2,1)}, bf16[40,2048]{1,0:T(8,128)(2,1)}) custom-call(bf16[256,512]{1,0:T(8,128)(2,1)} %states_hbm.1, s32[1,256]{1,0:T(1,128)} %bitcast.18, s32[2,40]{1,0:T(2,128)} %bitcast.19, f32[1,512]{1,0:T(1,128)} %bitcast.16, f32[1,2048]{1,0:T(1,128)} %bitcast.15, f32[1,512]{1,0:T(1,128)} %bitcast.17, f32[8,2048]{1,0:T(8,128)} %bitcast.14, ...), custom_call_target="tpu_custom_call" | custom-call | tf_op jit(solution)/shard_map/pallas_call | solution.py:620
  99.3 1.8 %shard_map.177 = (bf16[256,512]{1,0:T(8,128)(2,1)}, bf16[40,2048]{1,0:T(8,128)(2,1)}) custom-call(bf16[256,512]{1,0:T(8,128)(2,1)} %get-tuple-element.4.bytes_in, bf16[40,2048]{1,0:T(8,128)(2,1)} %get-tuple-element.5.patches_in), custom_call_target="tpu_custom_call" | custom-call | tf_op jit(solution)/shard_map/pallas_call | solution.py:661

commit v7 on v6

--- a/solution.py
+++ b/solution.py
@@ -16,6 +16,7 @@
 LAGS = (0, 2)
 PIECES = 2
 PASS_AT = 1
+AHEAD = 0
 SEQ = ("seq_0", "seq_1")
 SEQ_EXPERT = ("seq_0", "seq_1", "expert")
 
@@ -514,18 +515,20 @@
         return copies
 
     to_right, to_left = forward_right(1), forward_left(1)
-    landed_all(up_second)
-    fill_hidden(0)
     back = []
-    for tick in range(LAGS[-1] + ring):
-        hop = tick + 1
+    for turn in range(AHEAD + LAGS[-1] + ring):
+        hop, tick = turn + 1, turn - AHEAD
         if hop <= half:
             landed_all([to_right, to_left])
             if hop < half:
                 to_right, to_left = forward_right(hop + 1), forward_left(hop + 1)
+            if hop == 1:
+                landed_all(up_second)
             fill_hidden(hop)
             if hop < half:
                 fill_hidden(ring - hop)
+            else:
+                fill_hidden(0)
         if tick in LAGS:
             landed_all(down_second)
         if tick == PASS_AT:

time: 101 us -> 101 us (level)
  no operation moved by 1% of the time
where the time goes in v7:
time: 101 us
  Pallas kernels  100 us (99%)
    pallas_call x1, Pallas kernels, per_device(): pl.pallas_call(functools.partial(step_kernel, (groups, ring, peers)), out...  98.6 us

profile of v7, /device:TPU:1, one launch (start us, length us, event | category | flops | bytes accessed | tf_op | source)
XLA Modules:
  0.0 101.1 jit_solution(7256759568313465045)
XLA Ops:
  0.6 98.6 %shard_map.176 = (bf16[256,512]{1,0:T(8,128)(2,1)}, bf16[40,2048]{1,0:T(8,128)(2,1)}) custom-call(bf16[256,512]{1,0:T(8,128)(2,1)} %states_hbm.1, s32[1,256]{1,0:T(1,128)} %bitcast.18, s32[2,40]{1,0:T(2,128)} %bitcast.19, f32[1,512]{1,0:T(1,128)} %bitcast.16, f32[1,2048]{1,0:T(1,128)} %bitcast.15, f32[1,512]{1,0:T(1,128)} %bitcast.17, f32[8,2048]{1,0:T(8,128)} %bitcast.14, ...), custom_call_target="tpu_custom_call" | custom-call | tf_op jit(solution)/shard_map/pallas_call | solution.py:623
  99.3 1.8 %shard_map.177 = (bf16[256,512]{1,0:T(8,128)(2,1)}, bf16[40,2048]{1,0:T(8,128)(2,1)}) custom-call(bf16[256,512]{1,0:T(8,128)(2,1)} %get-tuple-element.4.bytes_in, bf16[40,2048]{1,0:T(8,128)(2,1)} %get-tuple-element.5.patches_in), custom_call_target="tpu_custom_call" | custom-call | tf_op jit(solution)/shard_map/pallas_call | solution.py:664
